TPU v7x, 32 devices: a whole 2x2x4 slice. The times are simulated.
32 devices in a mesh: groups: 2 (over y), hours: 4 (over z), years: 2 (over x), lines: 2 (over core).
Axes of the slice: x: 2, y: 2, z: 4, core: 2. Of those that a mesh axis runs over, the one named last changes fastest.
Arguments:
- demand: bfloat16 [8, 4, 2048], P(('groups', 'years'), 'hours'), parts along dimension 0, may hold values from 0.19921875 to 0.796875
- avail: bfloat16 [8, 4, 4096], P(('groups', 'years'), 'hours', 'lines'), parts along dimension 0, may hold values from 0.099609375 to 1
- ptdf: bfloat16 [1536, 2048], P('lines'), may hold values from -0.125 to 0.125
- line_limit: float32 [1536], P('lines'), may hold values from 0.3 to 3
- gen_cost: float32 [4096], P('lines'), may hold values from 0.2 to 5
- gen_cap: float32 [4096], P('lines'), may hold values from 0.3 to 1.5
- gen_node: int32 [4096], P('lines'), may hold values from 0 to 2047
- store_node: int32 [8192], P('lines'), may hold values from 0 to 2047
- store_power: float32 [8192], P('lines'), may hold values from 0.2 to 1
- capex: float32 [8192], P('lines'), may hold values from 0.05 to 1
- gen_state: float32 [8, 4, 4096], P(('groups', 'years'), 'hours', 'lines'), parts along dimension 0, may hold values from 0 to 0.6
- store_state: float32 [8, 4, 8192], P(('groups', 'years'), 'hours', 'lines'), parts along dimension 0, may hold values from -0.5 to 0.5
- level_upper: float32 [8, 4, 8192], P(('groups', 'years'), 'hours', 'lines'), parts along dimension 0, may hold values from 0 to 9, as said below
- level_lower: float32 [8, 4, 8192], P(('groups', 'years'), 'hours', 'lines'), parts along dimension 0, may hold values from 0 to 0.5
- flow_dual: float32 [8, 4, 1536], P(('groups', 'years'), 'hours', 'lines'), parts along dimension 0, may hold values from -3 to 3
- balance_dual: float32 [8, 4], P(('groups', 'years'), 'hours'), parts along dimension 0, may hold values from -6 to 6
- capacity: float32 [16384], P(('groups', 'lines')), parts along dimension 0, may hold values from 0.05 to 2
Outputs:
- gen_next: float32 [8, 4, 4096], P(('groups', 'years'), 'hours', 'lines'), parts along dimension 0
- store_next: float32 [8, 4, 8192], P(('groups', 'years'), 'hours', 'lines'), parts along dimension 0
- capacity_next: float32 [16384], P(('groups', 'lines')), parts along dimension 0
- balance_next: float32 [8, 4], P(('groups', 'years'), 'hours'), parts along dimension 0
- flow_next: float32 [8, 4, 1536], P(('groups', 'years'), 'hours', 'lines'), parts along dimension 0
- upper_next: float32 [8, 4, 8192], P(('groups', 'years'), 'hours', 'lines'), parts along dimension 0
- lower_next: float32 [8, 4, 8192], P(('groups', 'years'), 'hours', 'lines'), parts along dimension 0
There are 2 independent parts, one for each index of `groups`. A program takes and returns all parts, laid end to end along the dimension named above; an argument that names none is the same for every part. Nothing has to cross between parts.
Inputs may be any that keep to these rules, and one draw needn't show every extreme that they name: `level_upper`: nonnegative.
All inputs are finite; a program needn't handle non-finite values.
Results may differ from a plain program's by a relative error of at most 0.004.
Values may be sent and summed in bfloat16 or wider, within the bound.
A program may use at most 64 MiB of HBM per device.

v0:
```python
import functools
import math

import jax
import jax.numpy as jnp
from jax import lax
from jax.experimental import pallas as pl
from jax.experimental.pallas import tpu as pltpu
from jax.sharding import PartitionSpec as P

TAU = 0.1
SIGMA = 0.5
TAU_CAP = 1.0
LANES = 128
SPLITS = 2
LINK = jnp.bfloat16
MESH = pl.DeviceIdType.MESH


def step_kernel(
    sizes,
    demand_h, avail_h, ptdf_h, limit_h, cost_h, cap_h, gnode_h, snode_h, power_h,
    capex_h, gen_h, store_h, upper_h, lower_h, flow_h, capacity_h, balance_h,
    gen_w, store_w, capacity_w, flow_w, upper_w, lower_w, balance_o,
    demand_v, avail_v, ptdf_v, limit_v, cost_v, cap_v, gnode_v, snode_v, power_v,
    capex_v, gen_v, store_v, upper_v, lower_v, flow_v, capacity_v, balance_v,
    flow8, limit1, net_s, net_r, inj_s, inj_r, inj8, avail_d, demand_d,
    dual_s, dual_r, up_s, up_r, year_s, year_r, bar_s, bar_r, suffix_v, level_v,
    gbar_v, sbar_v, price_v, spread, onehot, highhot,
    in_sem, net_sem, inj_sem, dual_sem, up_sem, year_sem, bar_sem,
):
    years_dev, hours_dev, hours, years, level_scale, node_scale, hour_count = sizes
    rows = years_dev * hours_dev
    me_h, me_y, me_l = lax.axis_index("hours"), lax.axis_index("years"), lax.axis_index("lines")
    nodes = ptdf_v.shape[1]
    hi_count = nodes // LANES
    line_local = ptdf_v.shape[0]
    gen_rows, store_rows = gnode_v.shape[0], snode_v.shape[0]
    link = dual_s.dtype

    order = (
        (upper_h, upper_v), (lower_h, lower_v), (snode_h, snode_v), (gnode_h, gnode_v),
        (flow_h, flow_v), (ptdf_h, ptdf_v), (store_h, store_v), (power_h, power_v),
        (gen_h, gen_v), (cost_h, cost_v), (cap_h, cap_v), (avail_h, avail_v),
        (demand_h, demand_v), (limit_h, limit_v), (capex_h, capex_v), (capacity_h, capacity_v),
        (balance_h, balance_v),
    )
    loads = [pltpu.make_async_copy(s, d, in_sem.at[i]) for i, (s, d) in enumerate(order)]

    def hour_peer(k):
        return {"hours": lax.rem(me_h + k, hours)}

    def year_peer(k):
        return {"years": lax.rem(me_y + k, years)}

    partner = {"lines": 1 - me_l}
    barrier = pltpu.get_barrier_semaphore()
    peers = [partner] + [hour_peer(k) for k in range(1, hours)] + [year_peer(k) for k in range(1, years)]
    for peer in peers:
        pl.semaphore_signal(barrier, inc=1, device_id=peer, device_id_type=MESH)
    for copy in loads:
        copy.start()

    loads[0].wait()
    loads[1].wait()
    local_upper = None
    for y in range(years_dev):
        total = None
        for h in range(hours_dev):
            r = y * hours_dev + h
            diff = upper_v[r] - lower_v[r]
            total = diff if total is None else total + diff
            local_upper = upper_v[r] if local_upper is None else local_upper + upper_v[r]
        dual_s[y] = total.astype(link)
    year_s[...] = local_upper

    pl.semaphore_wait(barrier, len(peers))

    def remote(src, dst, sem, k, peer):
        return pltpu.make_async_remote_copy(
            src_ref=src, dst_ref=dst, send_sem=sem.at[0, k], recv_sem=sem.at[1, k],
            device_id=peer, device_id_type=MESH,
        )

    def dual_copy(k):
        return remote(dual_s, dual_r.at[k - 1], dual_sem, k - 1, hour_peer(hours - k))

    def bar_copy(k):
        return remote(bar_s, bar_r.at[k - 1], bar_sem, k - 1, hour_peer(k))

    ups = [remote(up_s, up_r.at[k - 1], up_sem, k - 1, hour_peer(k)) for k in range(1, hours)]
    year_copies = [remote(year_s, year_r.at[k - 1], year_sem, k - 1, year_peer(k)) for k in range(1, years)]
    net_copy = remote(net_s, net_r, net_sem, 0, partner)
    inj_copy = remote(inj_s, inj_r, inj_sem, 0, partner)

    for k in range(hours - 1, 0, -1):
        @pl.when(me_h >= k)
        def _(k=k):
            dual_copy(k).start()
    for copy in year_copies:
        copy.start()

    loads[4].wait()
    flow8[...] = jnp.zeros_like(flow8)
    for r in range(rows):
        flow8[r : r + 1, :] = flow_v[r]
    dual_half = flow8[...].astype(jnp.bfloat16)
    loads[5].wait()
    net = jnp.dot(dual_half, ptdf_v[...], preferred_element_type=jnp.float32)
    net_s[...] = net[:rows]
    net_copy.start()

    for copy in year_copies:
        copy.wait_recv()
    block_upper = year_s[...]
    for k in range(1, years):
        block_upper = block_upper + year_r[k - 1]
    up_s[...] = block_upper
    for copy in reversed(ups):
        copy.start()

    loads[2].wait()
    loads[3].wait()
    high_rows = lax.broadcasted_iota(jnp.int32, (hi_count, LANES), 0)
    lane_rows = lax.broadcasted_iota(jnp.int32, (LANES, LANES), 0)

    def node_row(a):
        if a < store_rows:
            return snode_v[a : a + 1, :]
        return gnode_v[a - store_rows : a - store_rows + 1, :]

    for a in range(store_rows + gen_rows):
        low = jnp.broadcast_to(node_row(a) % LANES, (LANES, LANES))
        onehot[:, a * LANES : (a + 1) * LANES] = jnp.where(low == lane_rows, 1.0, 0.0).astype(jnp.bfloat16)
        high = jnp.broadcast_to(node_row(a) // LANES, (hi_count, LANES))
        highhot[:, a * LANES : (a + 1) * LANES] = jnp.where(high == high_rows, 1.0, 0.0).astype(jnp.bfloat16)

    for copy in loads[6:]:
        copy.wait()
    for r in range(rows):
        for j in range(hi_count):
            piece = slice(j * LANES, (j + 1) * LANES)
            demand_d[r, j : j + 1, :] = demand_v[r : r + 1, piece].astype(jnp.float32)
        for j in range(gen_rows):
            piece = slice(j * LANES, (j + 1) * LANES)
            avail_d[r, j : j + 1, :] = avail_v[r : r + 1, piece].astype(jnp.float32)

    net_copy.wait_recv()
    prices = net_s[...] + net_r[...]

    def gather(r, node):
        price_row = prices[r : r + 1] + node_scale * balance_v[:, r : r + 1]
        high, low = node // LANES, node % LANES
        result = jnp.zeros(node.shape, jnp.float32)
        for j in range(hi_count):
            table = jnp.broadcast_to(price_row[:, j * LANES : (j + 1) * LANES], node.shape)
            picked = jnp.take_along_axis(table, low, axis=1, mode="promise_in_bounds")
            result = jnp.where(high == j, picked, result)
        return result

    for r in range(rows):
        for b in range(0, store_rows, 8):
            price_v[r, b : b + 8] = gather(r, snode_v[b : b + 8])

    for r in range(rows):
        for b in range(0, gen_rows, 8):
            part = slice(b, b + 8)
            price = gather(r, gnode_v[part])
            new = gen_v[r, part] - TAU * (cost_v[part] + price)
            new = jnp.minimum(jnp.maximum(new, 0.0), cap_v[part] * avail_d[r, part])
            gen_w[r, part] = new
            gbar_v[r, part] = 2.0 * new - gen_v[r, part]

    def place(values, sign, first, count):
        for r in range(rows):
            rest = sign * values[r]
            for p in range(SPLITS):
                piece = rest.astype(jnp.bfloat16).astype(jnp.float32)
                rest = rest - piece
                base = (r * SPLITS + p) * hi_count
                for a in range(count):
                    cols = slice((first + a) * LANES, (first + a + 1) * LANES)
                    wide = jnp.broadcast_to(piece[a : a + 1], (hi_count, LANES)).astype(jnp.bfloat16)
                    spread[base : base + hi_count, cols] = wide * highhot[:, cols]
        cols = slice(first * LANES, (first + count) * LANES)
        return lax.dot_general(
            spread[:, cols], onehot[:, cols], (((1,), (1,)), ((), ())), preferred_element_type=jnp.float32
        )

    placed = place(gbar_v, 1.0, store_rows, gen_rows)

    for y in range(years_dev):
        suffix_v[y] = jnp.zeros_like(suffix_v[y])
    for k in range(1, hours):
        @pl.when(me_h + k < hours)
        def _(k=k):
            dual_copy(k).wait_recv()
            for y in range(years_dev):
                suffix_v[y] = suffix_v[y] + dual_r[k - 1, y].astype(jnp.float32)
    for y in range(years_dev):
        beyond = suffix_v[y]
        bar_total = jnp.zeros_like(beyond)
        for h in reversed(range(hours_dev)):
            r = y * hours_dev + h
            beyond = beyond + (upper_v[r] - lower_v[r])
            suffix = level_scale * beyond
            power = power_v[...]
            new = store_v[r] - TAU * (suffix - price_v[r])
            new = jnp.minimum(jnp.maximum(new, -power), power)
            store_w[r] = new
            sbar = 2.0 * new - store_v[r]
            sbar_v[r] = sbar
            bar_total = bar_total + sbar
        bar_s[y] = bar_total.astype(link)
    for k in range(hours - 1, 0, -1):
        @pl.when(me_h + k < hours)
        def _(k=k):
            bar_copy(k).start()
    placed = placed + place(sbar_v, -1.0, 0, store_rows)
    for r in range(rows):
        total = None
        for p in range(SPLITS):
            base = (r * SPLITS + p) * hi_count
            piece = placed[base : base + hi_count]
            total = piece if total is None else total + piece
        inj_s[r] = total
    inj_copy.start()

    for c in range(line_local // LANES):
        limit1[:, c * LANES : (c + 1) * LANES] = limit_v[c : c + 1, :]
    inj8[...] = jnp.zeros_like(inj8)

    inj_copy.wait_recv()
    for r in range(rows):
        inject = inj_s[r] + inj_r[r] - demand_d[r]
        balance_o[:, r : r + 1] = balance_v[:, r : r + 1] + SIGMA * node_scale * jnp.sum(inject, keepdims=True)
        for j in range(hi_count):
            inj8[r : r + 1, j * LANES : (j + 1) * LANES] = inject[j : j + 1]
    line_flows = lax.dot_general(
        inj8[...].astype(jnp.bfloat16), ptdf_v[...], (((1,), (1,)), ((), ())),
        preferred_element_type=jnp.float32,
    )
    shifted = flow8[...] + SIGMA * line_flows
    limit = limit1[...]
    line_next = shifted - SIGMA * jnp.minimum(jnp.maximum(shifted / SIGMA, -limit), limit)
    for r in range(rows):
        flow_w[r] = line_next[r : r + 1]

    for copy in ups:
        copy.wait_recv()
    upper_total = up_s[...]
    for k in range(1, hours):
        upper_total = upper_total + up_r[k - 1]
    capacity_next = jnp.maximum(capacity_v[...] - TAU_CAP * (capex_v[...] - upper_total / hour_count), 0.0)
    capacity_w[...] = capacity_next
    capacity_bar = 2.0 * capacity_next - capacity_v[...]

    for y in range(years_dev):
        level_v[y] = jnp.zeros_like(level_v[y])
    for k in range(1, hours):
        @pl.when(me_h >= k)
        def _(k=k):
            bar_copy(k).wait_recv()
            for y in range(years_dev):
                level_v[y] = level_v[y] + bar_r[k - 1, y].astype(jnp.float32)
    for y in range(years_dev):
        before = level_v[y]
        for h in range(hours_dev):
            r = y * hours_dev + h
            before = before + sbar_v[r]
            level = level_scale * before
            upper_w[r] = jnp.maximum(upper_v[r] + SIGMA * (level - capacity_bar), 0.0)
            lower_w[r] = jnp.maximum(lower_v[r] - SIGMA * level, 0.0)

    net_copy.wait_send()
    inj_copy.wait_send()
    for copy in ups + year_copies:
        copy.wait_send()
    for k in range(1, hours):
        @pl.when(me_h >= k)
        def _(k=k):
            dual_copy(k).wait_send()

        @pl.when(me_h + k < hours)
        def _(k=k):
            bar_copy(k).wait_send()


def finish_kernel(count, *refs):
    sources, targets, sem = refs[:count], refs[count : 2 * count], refs[2 * count]
    copies = [pltpu.make_async_copy(s, t, sem.at[i]) for i, (s, t) in enumerate(zip(sources, targets))]
    for copy in copies:
        copy.start()
    for copy in copies:
        copy.wait()


def local(
    demand, avail, ptdf, line_limit, gen_cost, gen_cap, gen_node, store_node, store_power,
    capex, gen_state, store_state, level_upper, level_lower, flow_dual, balance_dual, capacity,
):
    years_dev, hours_dev, nodes = demand.shape
    rows = years_dev * hours_dev
    hours, years = lax.axis_size("hours"), lax.axis_size("years")
    hours_total = hours_dev * hours
    hour_count = years_dev * years * hours_total
    level_scale = 1.0 / math.sqrt(hours_total)
    node_scale = 1.0 / math.sqrt(nodes)
    sizes = (years_dev, hours_dev, hours, years, level_scale, node_scale, hour_count)

    def fold(x):
        return x.reshape(-1, LANES)

    def fold_rows(x):
        return x.reshape(rows, -1, LANES)

    args = (
        demand.reshape(rows, nodes), avail.reshape(rows, -1), ptdf, fold(line_limit), fold(gen_cost),
        fold(gen_cap), fold(gen_node), fold(store_node), fold(store_power), fold(capex),
        fold_rows(gen_state), fold_rows(store_state), fold_rows(level_upper), fold_rows(level_lower),
        flow_dual.reshape(rows, 1, -1), fold(capacity), balance_dual.reshape(1, rows),
    )
    f32 = jnp.float32
    gen_rows, store_rows = args[6].shape[0], args[7].shape[0]
    line_local, hi_count = ptdf.shape[0], nodes // LANES
    padded = max(8, -(-rows // 8) * 8)
    out_shapes = [
        (rows, gen_rows, LANES), (rows, store_rows, LANES), (store_rows, LANES),
        (rows, 1, line_local), (rows, store_rows, LANES), (rows, store_rows, LANES),
    ]
    any_spec = pl.BlockSpec(memory_space=pl.ANY)
    block, blocks = (store_rows, LANES), (years_dev, store_rows, LANES)
    h1, y1 = max(hours - 1, 1), max(years - 1, 1)
    dma = pltpu.SemaphoreType.DMA
    scratch = [pltpu.VMEM(a.shape, a.dtype) for a in args]
    scratch += [
        pltpu.VMEM((padded, line_local), f32), pltpu.VMEM((1, line_local), f32),
        pltpu.VMEM((rows, nodes), f32), pltpu.VMEM((rows, nodes), f32),
        pltpu.VMEM((rows, hi_count, LANES), f32), pltpu.VMEM((rows, hi_count, LANES), f32),
        pltpu.VMEM((padded, nodes), f32), pltpu.VMEM((rows, gen_rows, LANES), f32),
        pltpu.VMEM((rows, hi_count, LANES), f32),
        pltpu.VMEM(blocks, LINK), pltpu.VMEM((h1,) + blocks, LINK),
        pltpu.VMEM(block, f32), pltpu.VMEM((h1,) + block, f32),
        pltpu.VMEM(block, f32), pltpu.VMEM((y1,) + block, f32),
        pltpu.VMEM(blocks, LINK), pltpu.VMEM((h1,) + blocks, LINK),
        pltpu.VMEM(blocks, f32), pltpu.VMEM(blocks, f32),
        pltpu.VMEM((rows, gen_rows, LANES), f32), pltpu.VMEM((rows, store_rows, LANES), f32),
        pltpu.VMEM((rows, store_rows, LANES), f32),
        pltpu.VMEM((rows * SPLITS * hi_count, (gen_rows + store_rows) * LANES), jnp.bfloat16),
        pltpu.VMEM((LANES, (gen_rows + store_rows) * LANES), jnp.bfloat16),
        pltpu.VMEM((hi_count, (gen_rows + store_rows) * LANES), jnp.bfloat16),
        dma((17,)), dma((2, 1)), dma((2, 1)), dma((2, h1)), dma((2, h1)), dma((2, y1)), dma((2, h1)),
    ]
    results = pl.pallas_call(
        functools.partial(step_kernel, sizes),
        out_shape=[pltpu.VMEM(s, f32) for s in out_shapes] + [pltpu.VMEM((1, rows), f32)],
        in_specs=[any_spec] * 17,
        out_specs=[pl.BlockSpec(memory_space=pltpu.VMEM)] * 7,
        scratch_shapes=scratch,
        compiler_params=pltpu.CompilerParams(
            collective_id=0, has_side_effects=True, vmem_limit_bytes=56 * 1024 * 1024
        ),
    )(*args)
    gen, store, cap, flow, upper, lower, balance = pl.pallas_call(
        functools.partial(finish_kernel, len(results)),
        out_shape=[jax.ShapeDtypeStruct(x.shape, f32) for x in results],
        in_specs=[pl.BlockSpec(memory_space=pltpu.VMEM)] * len(results),
        out_specs=[any_spec] * len(results),
        scratch_shapes=[dma((len(results),))],
    )(*[pltpu.with_memory_space_constraint(x, pltpu.VMEM) for x in results])
    return (
        gen.reshape(gen_state.shape), store.reshape(store_state.shape), cap.reshape(capacity.shape),
        balance.reshape(balance_dual.shape), flow.reshape(flow_dual.shape),
        upper.reshape(level_upper.shape), lower.reshape(level_lower.shape),
    )


def solution(mesh):
    row = P(("groups", "years"), "hours", "lines")
    line = P("lines")
    in_specs = (
        P(("groups", "years"), "hours", None), row, P("lines", None), line, line, line, line, line,
        line, line, row, row, row, row, row, P(("groups", "years"), "hours"), P(("groups", "lines")),
    )
    out_specs = (row, row, P(("groups", "lines")), P(("groups", "years"), "hours"), row, row, row)
    return jax.shard_map(local, mesh=mesh, in_specs=in_specs, out_specs=out_specs, check_vma=False)
```

profile of v0, /device:TPU:1, one launch (start us, length us, event | category | flops | bytes accessed | tf_op | source)
XLA Modules:
  0.0 14.7 jit_solution(16017638154802551372)
XLA Ops:
  0.6 13.3 %shard_map.216 = (f32[2,16,128]{2,1,0:T(8,128)S(1)}, f32[2,32,128]{2,1,0:T(8,128)S(1)}, f32[32,128]{1,0:T(8,128)S(1)}, f32[2,1,768]{2,1,0:T(1,128)S(1)}, f32[2,3...) custom-call(bf16[2,2048]{1,0:T(2,128)(2,1)} %bitcast.29, bf16[2,2048]{1,0:T(2,128)(2,1)} %bitcast.30, ...), custom_call_target="tpu_custom_call" | custom-call | tf_op jit(solution)/shard_map/pallas_call | solution.py:354
  14.0 0.7 %shard_map.217 = (f32[2,16,128]{2,1,0:T(8,128)}, f32[2,32,128]{2,1,0:T(8,128)}, f32[32,128]{1,0:T(8,128)}, f32[2,1,768]{2,1,0:T(1,128)}, f32[2,32,128]{2,1,0:T(8...) custom-call(f32[2,16,128]{2,1,0:T(8,128)S(1)} %get-tuple-element.21.refs_0_, f32[2,32,128]{2,1,0:T(8,128)S(1)} %get-tuple-element.22.refs_1_, ...), custom_call_target="tpu_custom_call" | custom-call | tf_op jit(solution)/shard_map/pallas_call | solution.py:364
where the time goes:
time: 14.8 us; the launch traced here: 14.7 us
  Pallas kernels  14 us (95%)
  between operations  0.65 us (4%)
    pallas_call x1, Pallas kernels, local(): pl.pallas_call(functools.partial(step_kernel, sizes), out_shape=[pltpu.VM...  13.3 us
    pallas_call x1, Pallas kernels, local(): pl.pallas_call(functools.partial(finish_kernel, len(results)), out_shape=...  0.72 us

commit v1 on v0

--- a/solution.py
+++ b/solution.py
@@ -26,8 +26,8 @@
     capex_v, gen_v, store_v, upper_v, lower_v, flow_v, capacity_v, balance_v,
     flow8, limit1, net_s, net_r, inj_s, inj_r, inj8, avail_d, demand_d,
     dual_s, dual_r, up_s, up_r, year_s, year_r, bar_s, bar_r, suffix_v, level_v,
-    gbar_v, sbar_v, price_v, spread, onehot, highhot,
-    in_sem, net_sem, inj_sem, dual_sem, up_sem, year_sem, bar_sem,
+    gbar_v, sbar_v, price_v, spread, onehot, highhot, placed_v, sent, loaded,
+    in_sem, send_sem, recv_sem,
 ):
     years_dev, hours_dev, hours, years, level_scale, node_scale, hour_count = sizes
     rows = years_dev * hours_dev
@@ -39,13 +39,15 @@
     link = dual_s.dtype
 
     order = (
-        (upper_h, upper_v), (lower_h, lower_v), (snode_h, snode_v), (gnode_h, gnode_v),
-        (flow_h, flow_v), (ptdf_h, ptdf_v), (store_h, store_v), (power_h, power_v),
-        (gen_h, gen_v), (cost_h, cost_v), (cap_h, cap_v), (avail_h, avail_v),
-        (demand_h, demand_v), (limit_h, limit_v), (capex_h, capex_v), (capacity_h, capacity_v),
-        (balance_h, balance_v),
-    )
-    loads = [pltpu.make_async_copy(s, d, in_sem.at[i]) for i, (s, d) in enumerate(order)]
+        (upper_h, upper_v, 0), (lower_h, lower_v, 0), (flow_h, flow_v, 1), (ptdf_h, ptdf_v, 1),
+        (snode_h, snode_v, 2), (gnode_h, gnode_v, 2), (store_h, store_v, 2), (power_h, power_v, 2),
+        (gen_h, gen_v, 2), (cost_h, cost_v, 2), (cap_h, cap_v, 2), (avail_h, avail_v, 2),
+        (demand_h, demand_v, 2), (limit_h, limit_v, 2), (capex_h, capex_v, 2), (capacity_h, capacity_v, 2),
+        (balance_h, balance_v, 2),
+    )
+    loads = [pltpu.make_async_copy(s, d, in_sem.at[i]) for s, d, i in order]
+    for copy in loads:
+        copy.start()
 
     def hour_peer(k):
         return {"hours": lax.rem(me_h + k, hours)}
@@ -55,11 +57,19 @@
 
     partner = {"lines": 1 - me_l}
     barrier = pltpu.get_barrier_semaphore()
-    peers = [partner] + [hour_peer(k) for k in range(1, hours)] + [year_peer(k) for k in range(1, years)]
-    for peer in peers:
+
+    def ready(peer):
         pl.semaphore_signal(barrier, inc=1, device_id=peer, device_id_type=MESH)
-    for copy in loads:
-        copy.start()
+
+    dual_r[...] = jnp.zeros_like(dual_r)
+    bar_r[...] = jnp.zeros_like(bar_r)
+    ready(partner)
+    for k in range(1, years):
+        ready(year_peer(k))
+    for k in range(1, hours):
+        @pl.when(me_h + k < hours)
+        def _(k=k):
+            ready(hour_peer(k))
 
     loads[0].wait()
     loads[1].wait()
@@ -74,24 +84,29 @@
         dual_s[y] = total.astype(link)
     year_s[...] = local_upper
 
-    pl.semaphore_wait(barrier, len(peers))
-
-    def remote(src, dst, sem, k, peer):
+    pl.semaphore_wait(barrier, years + me_h)
+
+    def remote(src, dst, sem, peer):
         return pltpu.make_async_remote_copy(
-            src_ref=src, dst_ref=dst, send_sem=sem.at[0, k], recv_sem=sem.at[1, k],
+            src_ref=src, dst_ref=dst, send_sem=send_sem, recv_sem=recv_sem.at[sem],
             device_id=peer, device_id_type=MESH,
         )
 
+    def arrive(ref, sem):
+        pltpu.make_async_copy(ref, ref, sem).wait()
+
     def dual_copy(k):
-        return remote(dual_s, dual_r.at[k - 1], dual_sem, k - 1, hour_peer(hours - k))
+        return remote(dual_s, dual_r.at[k - 1], 2, hour_peer(hours - k))
 
     def bar_copy(k):
-        return remote(bar_s, bar_r.at[k - 1], bar_sem, k - 1, hour_peer(k))
-
-    ups = [remote(up_s, up_r.at[k - 1], up_sem, k - 1, hour_peer(k)) for k in range(1, hours)]
-    year_copies = [remote(year_s, year_r.at[k - 1], year_sem, k - 1, year_peer(k)) for k in range(1, years)]
-    net_copy = remote(net_s, net_r, net_sem, 0, partner)
-    inj_copy = remote(inj_s, inj_r, inj_sem, 0, partner)
+        return remote(bar_s, bar_r.at[k - 1], 3, hour_peer(k))
+
+    def up_copy(k):
+        return remote(up_s, up_r.at[k - 1], 4, hour_peer(k))
+
+    year_copies = [remote(year_s, year_r.at[k - 1], 5, year_peer(k)) for k in range(1, years)]
+    net_copy = remote(net_s, net_r, 0, partner)
+    inj_copy = remote(inj_s, inj_r, 1, partner)
 
     for k in range(hours - 1, 0, -1):
         @pl.when(me_h >= k)
@@ -100,27 +115,18 @@
     for copy in year_copies:
         copy.start()
 
-    loads[4].wait()
+    loads[2].wait()
+    loads[3].wait()
     flow8[...] = jnp.zeros_like(flow8)
     for r in range(rows):
         flow8[r : r + 1, :] = flow_v[r]
     dual_half = flow8[...].astype(jnp.bfloat16)
-    loads[5].wait()
     net = jnp.dot(dual_half, ptdf_v[...], preferred_element_type=jnp.float32)
     net_s[...] = net[:rows]
     net_copy.start()
 
-    for copy in year_copies:
-        copy.wait_recv()
-    block_upper = year_s[...]
-    for k in range(1, years):
-        block_upper = block_upper + year_r[k - 1]
-    up_s[...] = block_upper
-    for copy in reversed(ups):
-        copy.start()
-
-    loads[2].wait()
-    loads[3].wait()
+    for copy in loads[4:]:
+        copy.wait()
     high_rows = lax.broadcasted_iota(jnp.int32, (hi_count, LANES), 0)
     lane_rows = lax.broadcasted_iota(jnp.int32, (LANES, LANES), 0)
 
@@ -135,8 +141,6 @@
         high = jnp.broadcast_to(node_row(a) // LANES, (hi_count, LANES))
         highhot[:, a * LANES : (a + 1) * LANES] = jnp.where(high == high_rows, 1.0, 0.0).astype(jnp.bfloat16)
 
-    for copy in loads[6:]:
-        copy.wait()
     for r in range(rows):
         for j in range(hi_count):
             piece = slice(j * LANES, (j + 1) * LANES)
@@ -144,6 +148,16 @@
         for j in range(gen_rows):
             piece = slice(j * LANES, (j + 1) * LANES)
             avail_d[r, j : j + 1, :] = avail_v[r : r + 1, piece].astype(jnp.float32)
+
+    arrive(year_r, recv_sem.at[5])
+    block_upper = year_s[...]
+    for k in range(1, years):
+        block_upper = block_upper + year_r[k - 1]
+    up_s[...] = block_upper
+    for k in range(1, hours):
+        @pl.when(me_h + k >= hours)
+        def _(k=k):
+            up_copy(k).start()
 
     net_copy.wait_recv()
     prices = net_s[...] + net_r[...]
@@ -187,18 +201,16 @@
             spread[:, cols], onehot[:, cols], (((1,), (1,)), ((), ())), preferred_element_type=jnp.float32
         )
 
-    placed = place(gbar_v, 1.0, store_rows, gen_rows)
-
+    placed_v[...] = place(gbar_v, 1.0, store_rows, gen_rows)
+
+    for count in range(1, hours):
+        @pl.when(me_h + count == hours - 1)
+        def _(count=count):
+            arrive(dual_r.at[pl.ds(0, count)], recv_sem.at[2])
     for y in range(years_dev):
-        suffix_v[y] = jnp.zeros_like(suffix_v[y])
-    for k in range(1, hours):
-        @pl.when(me_h + k < hours)
-        def _(k=k):
-            dual_copy(k).wait_recv()
-            for y in range(years_dev):
-                suffix_v[y] = suffix_v[y] + dual_r[k - 1, y].astype(jnp.float32)
-    for y in range(years_dev):
-        beyond = suffix_v[y]
+        beyond = jnp.zeros_like(suffix_v[y])
+        for k in range(1, hours):
+            beyond = beyond + dual_r[k - 1, y].astype(jnp.float32)
         bar_total = jnp.zeros_like(beyond)
         for h in reversed(range(hours_dev)):
             r = y * hours_dev + h
@@ -216,7 +228,8 @@
         @pl.when(me_h + k < hours)
         def _(k=k):
             bar_copy(k).start()
-    placed = placed + place(sbar_v, -1.0, 0, store_rows)
+            up_copy(k).start()
+    placed = placed_v[...] + place(sbar_v, -1.0, 0, store_rows)
     for r in range(rows):
         total = None
         for p in range(SPLITS):
@@ -246,8 +259,7 @@
     for r in range(rows):
         flow_w[r] = line_next[r : r + 1]
 
-    for copy in ups:
-        copy.wait_recv()
+    arrive(up_r, recv_sem.at[4])
     upper_total = up_s[...]
     for k in range(1, hours):
         upper_total = upper_total + up_r[k - 1]
@@ -255,16 +267,14 @@
     capacity_w[...] = capacity_next
     capacity_bar = 2.0 * capacity_next - capacity_v[...]
 
+    for count in range(1, hours):
+        @pl.when(me_h == count)
+        def _(count=count):
+            arrive(bar_r.at[pl.ds(0, count)], recv_sem.at[3])
     for y in range(years_dev):
-        level_v[y] = jnp.zeros_like(level_v[y])
-    for k in range(1, hours):
-        @pl.when(me_h >= k)
-        def _(k=k):
-            bar_copy(k).wait_recv()
-            for y in range(years_dev):
-                level_v[y] = level_v[y] + bar_r[k - 1, y].astype(jnp.float32)
-    for y in range(years_dev):
-        before = level_v[y]
+        before = jnp.zeros_like(level_v[y])
+        for k in range(1, hours):
+            before = before + bar_r[k - 1, y].astype(jnp.float32)
         for h in range(hours_dev):
             r = y * hours_dev + h
             before = before + sbar_v[r]
@@ -272,23 +282,12 @@
             upper_w[r] = jnp.maximum(upper_v[r] + SIGMA * (level - capacity_bar), 0.0)
             lower_w[r] = jnp.maximum(lower_v[r] - SIGMA * level, 0.0)
 
-    net_copy.wait_send()
-    inj_copy.wait_send()
-    for copy in ups + year_copies:
-        copy.wait_send()
-    for k in range(1, hours):
-        @pl.when(me_h >= k)
-        def _(k=k):
-            dual_copy(k).wait_send()
-
-        @pl.when(me_h + k < hours)
-        def _(k=k):
-            bar_copy(k).wait_send()
+    arrive(sent, send_sem)
 
 
 def finish_kernel(count, *refs):
     sources, targets, sem = refs[:count], refs[count : 2 * count], refs[2 * count]
-    copies = [pltpu.make_async_copy(s, t, sem.at[i]) for i, (s, t) in enumerate(zip(sources, targets))]
+    copies = [pltpu.make_async_copy(s, t, sem) for s, t in zip(sources, targets)]
     for copy in copies:
         copy.start()
     for copy in copies:
@@ -332,6 +331,10 @@
     block, blocks = (store_rows, LANES), (years_dev, store_rows, LANES)
     h1, y1 = max(hours - 1, 1), max(years - 1, 1)
     dma = pltpu.SemaphoreType.DMA
+    block_size = store_rows * LANES * 4
+    sent_bytes = 8 * rows * nodes + (hours + years - 2) * block_size
+    sent_bytes += (hours - 1) * years_dev * store_rows * LANES * jnp.dtype(LINK).itemsize
+    sent_rows = sent_bytes // (4 * LANES)
     scratch = [pltpu.VMEM(a.shape, a.dtype) for a in args]
     scratch += [
         pltpu.VMEM((padded, line_local), f32), pltpu.VMEM((1, line_local), f32),
@@ -349,7 +352,9 @@
         pltpu.VMEM((rows * SPLITS * hi_count, (gen_rows + store_rows) * LANES), jnp.bfloat16),
         pltpu.VMEM((LANES, (gen_rows + store_rows) * LANES), jnp.bfloat16),
         pltpu.VMEM((hi_count, (gen_rows + store_rows) * LANES), jnp.bfloat16),
-        dma((17,)), dma((2, 1)), dma((2, 1)), dma((2, h1)), dma((2, h1)), dma((2, y1)), dma((2, h1)),
+        pltpu.VMEM((rows * SPLITS * hi_count, LANES), f32),
+        pltpu.VMEM((sent_rows, LANES), f32), pltpu.VMEM((8, LANES), f32),
+        dma((3,)), dma, dma((6,)),
     ]
     results = pl.pallas_call(
         functools.partial(step_kernel, sizes),
@@ -366,7 +371,7 @@
         out_shape=[jax.ShapeDtypeStruct(x.shape, f32) for x in results],
         in_specs=[pl.BlockSpec(memory_space=pltpu.VMEM)] * len(results),
         out_specs=[any_spec] * len(results),
-        scratch_shapes=[dma((len(results),))],
+        scratch_shapes=[dma],
     )(*[pltpu.with_memory_space_constraint(x, pltpu.VMEM) for x in results])
     return (
         gen.reshape(gen_state.shape), store.reshape(store_state.shape), cap.reshape(capacity.shape),

time: 14.8 us -> 12.8 us (0.86)
  Pallas kernels: 14 us -> 12 us
    pallas_call x1, Pallas kernels: 13.3 us -> 11.3 us  [local(): pl.pallas_call(functools.partial(step_kernel, sizes), out_shape=[pltpu.VM...]
where the time goes in v1:
time: 12.8 us; the launch traced here: 12.6 us
  Pallas kernels  12 us (94%)
  between operations  0.65 us (5%)
    pallas_call x1, Pallas kernels, local(): pl.pallas_call(functools.partial(step_kernel, sizes), out_shape=[pltpu.VM...  11.3 us
    pallas_call x1, Pallas kernels, local(): pl.pallas_call(functools.partial(finish_kernel, len(results)), out_shape=...  0.66 us

profile of v1, /device:TPU:1, one launch (start us, length us, event | category | flops | bytes accessed | tf_op | source)
XLA Modules:
  0.0 12.6 jit_solution(943649776286425511)
XLA Ops:
  0.6 11.3 %shard_map.216 = (f32[2,16,128]{2,1,0:T(8,128)S(1)}, f32[2,32,128]{2,1,0:T(8,128)S(1)}, f32[32,128]{1,0:T(8,128)S(1)}, f32[2,1,768]{2,1,0:T(1,128)S(1)}, f32[2,3...) custom-call(bf16[2,2048]{1,0:T(2,128)(2,1)} %bitcast.29, bf16[2,2048]{1,0:T(2,128)(2,1)} %bitcast.30, ...), custom_call_target="tpu_custom_call" | custom-call | tf_op jit(solution)/shard_map/pallas_call | solution.py:359
  12.0 0.7 %shard_map.217 = (f32[2,16,128]{2,1,0:T(8,128)}, f32[2,32,128]{2,1,0:T(8,128)}, f32[32,128]{1,0:T(8,128)}, f32[2,1,768]{2,1,0:T(1,128)}, f32[2,32,128]{2,1,0:T(8...) custom-call(f32[2,16,128]{2,1,0:T(8,128)S(1)} %get-tuple-element.21.refs_0_, f32[2,32,128]{2,1,0:T(8,128)S(1)} %get-tuple-element.22.refs_1_, ...), custom_call_target="tpu_custom_call" | custom-call | tf_op jit(solution)/shard_map/pallas_call | solution.py:369

commit v2 on v1

--- a/solution.py
+++ b/solution.py
@@ -25,9 +25,9 @@
     demand_v, avail_v, ptdf_v, limit_v, cost_v, cap_v, gnode_v, snode_v, power_v,
     capex_v, gen_v, store_v, upper_v, lower_v, flow_v, capacity_v, balance_v,
     flow8, limit1, net_s, net_r, inj_s, inj_r, inj8, avail_d, demand_d,
-    dual_s, dual_r, up_s, up_r, year_s, year_r, bar_s, bar_r, suffix_v, level_v,
-    gbar_v, sbar_v, price_v, spread, onehot, highhot, placed_v, sent, loaded,
-    in_sem, send_sem, recv_sem,
+    dual_s, dual_r, total_v, cross_r, above_s, above_r, bar_s, bar_r,
+    gbar_v, sbar_v, price_v, spread, onehot, highhot, placed_v, sent,
+    in_sem, send_sem, recv_sem, year_ready,
 ):
     years_dev, hours_dev, hours, years, level_scale, node_scale, hour_count = sizes
     rows = years_dev * hours_dev
@@ -37,6 +37,8 @@
     line_local = ptdf_v.shape[0]
     gen_rows, store_rows = gnode_v.shape[0], snode_v.shape[0]
     link = dual_s.dtype
+    block_rows = store_rows * link.itemsize // 4
+    base_rows = 2 * rows * hi_count + ((hours - 1) * (years_dev + 1) + years - 1) * block_rows
 
     order = (
         (upper_h, upper_v, 0), (lower_h, lower_v, 0), (flow_h, flow_v, 1), (ptdf_h, ptdf_v, 1),
@@ -49,27 +51,38 @@
     for copy in loads:
         copy.start()
 
-    def hour_peer(k):
-        return {"hours": lax.rem(me_h + k, hours)}
-
-    def year_peer(k):
-        return {"years": lax.rem(me_y + k, years)}
+    def peer(k, j):
+        return {"hours": lax.rem(me_h + k, hours), "years": lax.rem(me_y + j, years)}
 
     partner = {"lines": 1 - me_l}
     barrier = pltpu.get_barrier_semaphore()
 
-    def ready(peer):
-        pl.semaphore_signal(barrier, inc=1, device_id=peer, device_id_type=MESH)
+    def ready(device):
+        pl.semaphore_signal(barrier, inc=1, device_id=device, device_id_type=MESH)
 
     dual_r[...] = jnp.zeros_like(dual_r)
     bar_r[...] = jnp.zeros_like(bar_r)
+    cross_r[...] = jnp.zeros_like(cross_r)
+    above_r[...] = jnp.zeros_like(above_r)
     ready(partner)
-    for k in range(1, years):
-        ready(year_peer(k))
     for k in range(1, hours):
         @pl.when(me_h + k < hours)
         def _(k=k):
-            ready(hour_peer(k))
+            ready(peer(k, 0))
+    for j in range(1, years):
+        @pl.when(me_y + j < years)
+        def _(j=j):
+            ready(peer(0, j))
+            for k in range(1, hours):
+                @pl.when(me_h + k < hours)
+                def _(k=k):
+                    ready(peer(k, j))
+
+    pl.semaphore_wait(barrier, 1 + me_y + me_h * (1 + me_y))
+    for j in range(1, years):
+        @pl.when(me_y + j >= years)
+        def _(j=j):
+            pl.semaphore_signal(year_ready, inc=1, device_id=peer(0, j), device_id_type=MESH)
 
     loads[0].wait()
     loads[1].wait()
@@ -82,29 +95,31 @@
             total = diff if total is None else total + diff
             local_upper = upper_v[r] if local_upper is None else local_upper + upper_v[r]
         dual_s[y] = total.astype(link)
-    year_s[...] = local_upper
-
-    pl.semaphore_wait(barrier, years + me_h)
-
-    def remote(src, dst, sem, peer):
+    dual_s[years_dev] = local_upper.astype(link)
+    total_v[...] = local_upper
+
+    def remote(src, dst, sem, device):
         return pltpu.make_async_remote_copy(
             src_ref=src, dst_ref=dst, send_sem=send_sem, recv_sem=recv_sem.at[sem],
-            device_id=peer, device_id_type=MESH,
+            device_id=device, device_id_type=MESH,
         )
 
     def arrive(ref, sem):
         pltpu.make_async_copy(ref, ref, sem).wait()
 
     def dual_copy(k):
-        return remote(dual_s, dual_r.at[k - 1], 2, hour_peer(hours - k))
+        return remote(dual_s, dual_r.at[k - 1], 2, peer(hours - k, 0))
 
     def bar_copy(k):
-        return remote(bar_s, bar_r.at[k - 1], 3, hour_peer(k))
-
-    def up_copy(k):
-        return remote(up_s, up_r.at[k - 1], 4, hour_peer(k))
-
-    year_copies = [remote(year_s, year_r.at[k - 1], 5, year_peer(k)) for k in range(1, years)]
+        return remote(bar_s, bar_r.at[k - 1], 3, peer(k, 0))
+
+    def cross_copy(k, j):
+        slot = cross_r.at[k, j - 1]
+        return remote(dual_s.at[years_dev], slot, 4 if k else 5, peer(hours - k, years - j))
+
+    def above_copy(j):
+        return remote(above_s, above_r.at[j - 1], 6, peer(0, j))
+
     net_copy = remote(net_s, net_r, 0, partner)
     inj_copy = remote(inj_s, inj_r, 1, partner)
 
@@ -112,8 +127,15 @@
         @pl.when(me_h >= k)
         def _(k=k):
             dual_copy(k).start()
-    for copy in year_copies:
-        copy.start()
+    for j in range(1, years):
+        @pl.when(me_y >= j)
+        def _(j=j):
+            cross_copy(0, j).start()
+    for j in range(1, years):
+        for k in range(hours - 1, 0, -1):
+            @pl.when(jnp.logical_and(me_h >= k, me_y >= j))
+            def _(k=k, j=j):
+                cross_copy(k, j).start()
 
     loads[2].wait()
     loads[3].wait()
@@ -124,6 +146,15 @@
     net = jnp.dot(dual_half, ptdf_v[...], preferred_element_type=jnp.float32)
     net_s[...] = net[:rows]
     net_copy.start()
+
+    @pl.when(me_y < years - 1)
+    def _():
+        pl.semaphore_wait(year_ready, years - 1 - me_y)
+
+    for j in range(1, years):
+        @pl.when(me_y + j < years)
+        def _(j=j):
+            cross_copy(0, years - j).start()
 
     for copy in loads[4:]:
         copy.wait()
@@ -148,16 +179,6 @@
         for j in range(gen_rows):
             piece = slice(j * LANES, (j + 1) * LANES)
             avail_d[r, j : j + 1, :] = avail_v[r : r + 1, piece].astype(jnp.float32)
-
-    arrive(year_r, recv_sem.at[5])
-    block_upper = year_s[...]
-    for k in range(1, years):
-        block_upper = block_upper + year_r[k - 1]
-    up_s[...] = block_upper
-    for k in range(1, hours):
-        @pl.when(me_h + k >= hours)
-        def _(k=k):
-            up_copy(k).start()
 
     net_copy.wait_recv()
     prices = net_s[...] + net_r[...]
@@ -203,15 +224,26 @@
 
     placed_v[...] = place(gbar_v, 1.0, store_rows, gen_rows)
 
+    arrive(cross_r.at[0], recv_sem.at[5])
+    hour_upper = total_v[...]
+    for j in range(1, years):
+        hour_upper = hour_upper + cross_r[0, j - 1].astype(jnp.float32)
+    total_v[...] = hour_upper
+    bar_s[years_dev] = hour_upper.astype(link)
+
     for count in range(1, hours):
         @pl.when(me_h + count == hours - 1)
         def _(count=count):
             arrive(dual_r.at[pl.ds(0, count)], recv_sem.at[2])
+    above = dual_r[0, years_dev].astype(jnp.float32)
+    for k in range(2, hours):
+        above = above + dual_r[k - 1, years_dev].astype(jnp.float32)
+    above_s[...] = above.astype(link)
     for y in range(years_dev):
-        beyond = jnp.zeros_like(suffix_v[y])
-        for k in range(1, hours):
+        beyond = dual_r[0, y].astype(jnp.float32)
+        for k in range(2, hours):
             beyond = beyond + dual_r[k - 1, y].astype(jnp.float32)
-        bar_total = jnp.zeros_like(beyond)
+        bar_total = None
         for h in reversed(range(hours_dev)):
             r = y * hours_dev + h
             beyond = beyond + (upper_v[r] - lower_v[r])
@@ -222,13 +254,17 @@
             store_w[r] = new
             sbar = 2.0 * new - store_v[r]
             sbar_v[r] = sbar
-            bar_total = bar_total + sbar
+            bar_total = sbar if bar_total is None else bar_total + sbar
         bar_s[y] = bar_total.astype(link)
     for k in range(hours - 1, 0, -1):
         @pl.when(me_h + k < hours)
         def _(k=k):
             bar_copy(k).start()
-            up_copy(k).start()
+    for j in range(1, years):
+        @pl.when(jnp.logical_and(me_h < hours - 1, me_y + j < years))
+        def _(j=j):
+            above_copy(j).start()
+    total_v[...] = total_v[...] + above
     placed = placed_v[...] + place(sbar_v, -1.0, 0, store_rows)
     for r in range(rows):
         total = None
@@ -255,25 +291,37 @@
     )
     shifted = flow8[...] + SIGMA * line_flows
     limit = limit1[...]
-    line_next = shifted - SIGMA * jnp.minimum(jnp.maximum(shifted / SIGMA, -limit), limit)
+    line_next = shifted - SIGMA * jnp.minimum(jnp.maximum(shifted * (1.0 / SIGMA), -limit), limit)
     for r in range(rows):
         flow_w[r] = line_next[r : r + 1]
 
-    arrive(up_r, recv_sem.at[4])
-    upper_total = up_s[...]
-    for k in range(1, hours):
-        upper_total = upper_total + up_r[k - 1]
-    capacity_next = jnp.maximum(capacity_v[...] - TAU_CAP * (capex_v[...] - upper_total / hour_count), 0.0)
-    capacity_w[...] = capacity_next
-    capacity_bar = 2.0 * capacity_next - capacity_v[...]
-
+    for j in range(1, years):
+        for k in range(1, hours):
+            @pl.when(jnp.logical_and(me_h + k == hours - 1, me_y + j == years - 1))
+            def _(k=k, j=j):
+                arrive(cross_r.at[pl.ds(1, k), pl.ds(0, j)], recv_sem.at[4])
+
+        @pl.when(jnp.logical_and(me_h < hours - 1, me_y == j))
+        def _(j=j):
+            arrive(above_r.at[pl.ds(0, j)], recv_sem.at[6])
     for count in range(1, hours):
         @pl.when(me_h == count)
         def _(count=count):
             arrive(bar_r.at[pl.ds(0, count)], recv_sem.at[3])
+    upper_total = total_v[...]
+    for k in range(1, hours):
+        upper_total = upper_total + bar_r[k - 1, years_dev].astype(jnp.float32)
+        for j in range(1, years):
+            upper_total = upper_total + cross_r[k, j - 1].astype(jnp.float32)
+    for j in range(1, years):
+        upper_total = upper_total + above_r[j - 1].astype(jnp.float32)
+    capacity_next = jnp.maximum(capacity_v[...] - TAU_CAP * (capex_v[...] - upper_total / hour_count), 0.0)
+    capacity_w[...] = capacity_next
+    capacity_bar = 2.0 * capacity_next - capacity_v[...]
+
     for y in range(years_dev):
-        before = jnp.zeros_like(level_v[y])
-        for k in range(1, hours):
+        before = bar_r[0, y].astype(jnp.float32)
+        for k in range(2, hours):
             before = before + bar_r[k - 1, y].astype(jnp.float32)
         for h in range(hours_dev):
             r = y * hours_dev + h
@@ -282,7 +330,13 @@
             upper_w[r] = jnp.maximum(upper_v[r] + SIGMA * (level - capacity_bar), 0.0)
             lower_w[r] = jnp.maximum(lower_v[r] - SIGMA * level, 0.0)
 
-    arrive(sent, send_sem)
+    for y in range(years):
+        for h in range(hours):
+            blocks = h * y + (years - 1 - y if h < hours - 1 else 0)
+
+            @pl.when(jnp.logical_and(me_h == h, me_y == y))
+            def _(blocks=blocks):
+                arrive(sent.at[pl.ds(0, base_rows + blocks * block_rows)], send_sem)
 
 
 def finish_kernel(count, *refs):
@@ -328,13 +382,11 @@
         (rows, 1, line_local), (rows, store_rows, LANES), (rows, store_rows, LANES),
     ]
     any_spec = pl.BlockSpec(memory_space=pl.ANY)
-    block, blocks = (store_rows, LANES), (years_dev, store_rows, LANES)
+    block, blocks = (store_rows, LANES), (years_dev + 1, store_rows, LANES)
     h1, y1 = max(hours - 1, 1), max(years - 1, 1)
     dma = pltpu.SemaphoreType.DMA
-    block_size = store_rows * LANES * 4
-    sent_bytes = 8 * rows * nodes + (hours + years - 2) * block_size
-    sent_bytes += (hours - 1) * years_dev * store_rows * LANES * jnp.dtype(LINK).itemsize
-    sent_rows = sent_bytes // (4 * LANES)
+    block_rows = store_rows * jnp.dtype(LINK).itemsize // 4
+    sent_rows = 2 * rows * hi_count + (hours - 1) * (years_dev + 1) * block_rows + (hours + 1) * years * block_rows
     scratch = [pltpu.VMEM(a.shape, a.dtype) for a in args]
     scratch += [
         pltpu.VMEM((padded, line_local), f32), pltpu.VMEM((1, line_local), f32),
@@ -343,18 +395,17 @@
         pltpu.VMEM((padded, nodes), f32), pltpu.VMEM((rows, gen_rows, LANES), f32),
         pltpu.VMEM((rows, hi_count, LANES), f32),
         pltpu.VMEM(blocks, LINK), pltpu.VMEM((h1,) + blocks, LINK),
-        pltpu.VMEM(block, f32), pltpu.VMEM((h1,) + block, f32),
-        pltpu.VMEM(block, f32), pltpu.VMEM((y1,) + block, f32),
+        pltpu.VMEM(block, f32), pltpu.VMEM((hours, y1) + block, LINK),
+        pltpu.VMEM(block, LINK), pltpu.VMEM((y1,) + block, LINK),
         pltpu.VMEM(blocks, LINK), pltpu.VMEM((h1,) + blocks, LINK),
-        pltpu.VMEM(blocks, f32), pltpu.VMEM(blocks, f32),
         pltpu.VMEM((rows, gen_rows, LANES), f32), pltpu.VMEM((rows, store_rows, LANES), f32),
         pltpu.VMEM((rows, store_rows, LANES), f32),
         pltpu.VMEM((rows * SPLITS * hi_count, (gen_rows + store_rows) * LANES), jnp.bfloat16),
         pltpu.VMEM((LANES, (gen_rows + store_rows) * LANES), jnp.bfloat16),
         pltpu.VMEM((hi_count, (gen_rows + store_rows) * LANES), jnp.bfloat16),
         pltpu.VMEM((rows * SPLITS * hi_count, LANES), f32),
-        pltpu.VMEM((sent_rows, LANES), f32), pltpu.VMEM((8, LANES), f32),
-        dma((3,)), dma, dma((6,)),
+        pltpu.VMEM((sent_rows, LANES), f32),
+        dma((3,)), dma, dma((7,)), pltpu.SemaphoreType.REGULAR,
     ]
     results = pl.pallas_call(
         functools.partial(step_kernel, sizes),

time: 12.8 us -> 12.1 us (0.945)
  Pallas kernels: 12 us -> 11.3 us
    pallas_call x1, Pallas kernels: 11.3 us -> 10.6 us  [local(): pl.pallas_call(functools.partial(step_kernel, sizes), out_shape=[pltpu.VM...]
where the time goes in v2:
time: 12.1 us; the launch traced here: 11.9 us
  Pallas kernels  11.3 us (93%)
  between operations  0.65 us (5%)
    pallas_call x1, Pallas kernels, local(): pl.pallas_call(functools.partial(step_kernel, sizes), out_shape=[pltpu.VM...  10.6 us
    pallas_call x1, Pallas kernels, local(): pl.pallas_call(functools.partial(finish_kernel, len(results)), out_shape=...  0.66 us

profile of v2, /device:TPU:1, one launch (start us, length us, event | category | flops | bytes accessed | tf_op | source)
XLA Modules:
  0.0 11.9 jit_solution(16282445597439333201)
XLA Ops:
  0.6 10.6 %shard_map.216 = (f32[2,16,128]{2,1,0:T(8,128)S(1)}, f32[2,32,128]{2,1,0:T(8,128)S(1)}, f32[32,128]{1,0:T(8,128)S(1)}, f32[2,1,768]{2,1,0:T(1,128)S(1)}, f32[2,3...) custom-call(bf16[2,2048]{1,0:T(2,128)(2,1)} %bitcast.29, bf16[2,2048]{1,0:T(2,128)(2,1)} %bitcast.30, ...), custom_call_target="tpu_custom_call" | custom-call | tf_op jit(solution)/shard_map/pallas_call | solution.py:410
  11.2 0.7 %shard_map.217 = (f32[2,16,128]{2,1,0:T(8,128)}, f32[2,32,128]{2,1,0:T(8,128)}, f32[32,128]{1,0:T(8,128)}, f32[2,1,768]{2,1,0:T(1,128)}, f32[2,32,128]{2,1,0:T(8...) custom-call(f32[2,16,128]{2,1,0:T(8,128)S(1)} %get-tuple-element.21.refs_0_, f32[2,32,128]{2,1,0:T(8,128)S(1)} %get-tuple-element.22.refs_1_, ...), custom_call_target="tpu_custom_call" | custom-call | tf_op jit(solution)/shard_map/pallas_call | solution.py:420

commit v3 on v2

--- a/solution.py
+++ b/solution.py
@@ -13,6 +13,8 @@
 TAU_CAP = 1.0
 LANES = 128
 SPLITS = 2
+TILE = 256
+THIN = 4
 LINK = jnp.bfloat16
 MESH = pl.DeviceIdType.MESH
 
@@ -24,7 +26,7 @@
     gen_w, store_w, capacity_w, flow_w, upper_w, lower_w, balance_o,
     demand_v, avail_v, ptdf_v, limit_v, cost_v, cap_v, gnode_v, snode_v, power_v,
     capex_v, gen_v, store_v, upper_v, lower_v, flow_v, capacity_v, balance_v,
-    flow8, limit1, net_s, net_r, inj_s, inj_r, inj8, avail_d, demand_d,
+    flow8, limit1, net_s, net_r, inj_s, inj_r, inj8, line8, avail_d, demand_d,
     dual_s, dual_r, total_v, cross_r, above_s, above_r, bar_s, bar_r,
     gbar_v, sbar_v, price_v, spread, onehot, highhot, placed_v, sent,
     in_sem, send_sem, recv_sem, year_ready,
@@ -32,16 +34,16 @@
     years_dev, hours_dev, hours, years, level_scale, node_scale, hour_count = sizes
     rows = years_dev * hours_dev
     me_h, me_y, me_l = lax.axis_index("hours"), lax.axis_index("years"), lax.axis_index("lines")
-    nodes = ptdf_v.shape[1]
-    hi_count = nodes // LANES
-    line_local = ptdf_v.shape[0]
+    hi_count, line_local = ptdf_v.shape[0], ptdf_v.shape[1]
+    padded = flow8.shape[0]
     gen_rows, store_rows = gnode_v.shape[0], snode_v.shape[0]
     link = dual_s.dtype
     block_rows = store_rows * link.itemsize // 4
     base_rows = 2 * rows * hi_count + ((hours - 1) * (years_dev + 1) + years - 1) * block_rows
 
     order = (
-        (upper_h, upper_v, 0), (lower_h, lower_v, 0), (flow_h, flow_v, 1), (ptdf_h, ptdf_v, 1),
+        (upper_h, upper_v, 0), (lower_h, lower_v, 0), (flow_h, flow_v, 1),
+    ) + tuple((ptdf_h.at[:, pl.ds(j * LANES, LANES)], ptdf_v.at[j], 1) for j in range(hi_count)) + (
         (snode_h, snode_v, 2), (gnode_h, gnode_v, 2), (store_h, store_v, 2), (power_h, power_v, 2),
         (gen_h, gen_v, 2), (cost_h, cost_v, 2), (cap_h, cap_v, 2), (avail_h, avail_v, 2),
         (demand_h, demand_v, 2), (limit_h, limit_v, 2), (capex_h, capex_v, 2), (capacity_h, capacity_v, 2),
@@ -50,6 +52,29 @@
     loads = [pltpu.make_async_copy(s, d, in_sem.at[i]) for s, d, i in order]
     for copy in loads:
         copy.start()
+
+    def wide(ref, first, count):
+        return jnp.concatenate([ref[first + i] for i in range(count)], axis=1)
+
+    def multiply(jobs, transpose):
+        stage = [0, 0]
+        for unit, acc, left, right in jobs:
+            pltpu.matmul_push_rhs(right, stage[unit], unit, transpose=transpose)
+            pltpu.matmul_acc_lhs(acc, left, load_staged_rhs=stage[unit])
+            stage[unit] = 1 - stage[unit]
+
+    def tile(i, rows_from):
+        rows_here = pl.ds(rows_from * TILE, TILE)
+        return jnp.concatenate([ptdf_v[2 * i, rows_here], ptdf_v[2 * i + 1, rows_here]], axis=1)
+
+    def scoped(height, count, body):
+        specs = [pltpu.ACC(mxu_id=i)((height, TILE), jnp.float32) for i in range(2) for _ in range(count)]
+        pl.run_scoped(lambda *accs: body((accs[:count], accs[count:])), *specs)
+
+    def cols(i):
+        return slice(i * TILE, (i + 1) * TILE)
+
+    node_tiles, line_tiles = hi_count * LANES // TILE, line_local // TILE
 
     def peer(k, j):
         return {"hours": lax.rem(me_h + k, hours), "years": lax.rem(me_y + j, years)}
@@ -137,14 +162,24 @@
             def _(k=k, j=j):
                 cross_copy(k, j).start()
 
-    loads[2].wait()
-    loads[3].wait()
+    for copy in loads[2 : 3 + hi_count]:
+        copy.wait()
     flow8[...] = jnp.zeros_like(flow8)
     for r in range(rows):
         flow8[r : r + 1, :] = flow_v[r]
     dual_half = flow8[...].astype(jnp.bfloat16)
-    net = jnp.dot(dual_half, ptdf_v[...], preferred_element_type=jnp.float32)
-    net_s[...] = net[:rows]
+    for first in range(0, node_tiles, 2 * THIN):
+        def nodes_group(accs, first=first):
+            group = range(first, min(first + 2 * THIN, node_tiles))
+            jobs = [
+                (n % 2, accs[n % 2][(n - first) // 2], dual_half[:, cols(k)], tile(n, k))
+                for base in group[::2] for k in range(line_tiles) for n in (base, base + 1) if n in group
+            ]
+            multiply(jobs, False)
+            for n in group:
+                net_s[:, cols(n)] = pltpu.matmul_pop(accs[n % 2][(n - first) // 2])[:rows]
+
+        scoped(padded, THIN, nodes_group)
     net_copy.start()
 
     @pl.when(me_y < years - 1)
@@ -156,7 +191,7 @@
         def _(j=j):
             cross_copy(0, years - j).start()
 
-    for copy in loads[4:]:
+    for copy in loads[3 + hi_count :]:
         copy.wait()
     high_rows = lax.broadcasted_iota(jnp.int32, (hi_count, LANES), 0)
     lane_rows = lax.broadcasted_iota(jnp.int32, (LANES, LANES), 0)
@@ -168,9 +203,9 @@
 
     for a in range(store_rows + gen_rows):
         low = jnp.broadcast_to(node_row(a) % LANES, (LANES, LANES))
-        onehot[:, a * LANES : (a + 1) * LANES] = jnp.where(low == lane_rows, 1.0, 0.0).astype(jnp.bfloat16)
+        onehot[a] = jnp.where(low == lane_rows, 1.0, 0.0).astype(jnp.bfloat16)
         high = jnp.broadcast_to(node_row(a) // LANES, (hi_count, LANES))
-        highhot[:, a * LANES : (a + 1) * LANES] = jnp.where(high == high_rows, 1.0, 0.0).astype(jnp.bfloat16)
+        highhot[a] = jnp.where(high == high_rows, 1.0, 0.0).astype(jnp.bfloat16)
 
     for r in range(rows):
         for j in range(hi_count):
@@ -206,7 +241,7 @@
             gen_w[r, part] = new
             gbar_v[r, part] = 2.0 * new - gen_v[r, part]
 
-    def place(values, sign, first, count):
+    def place(values, sign, first, count, start, target):
         for r in range(rows):
             rest = sign * values[r]
             for p in range(SPLITS):
@@ -214,15 +249,26 @@
                 rest = rest - piece
                 base = (r * SPLITS + p) * hi_count
                 for a in range(count):
-                    cols = slice((first + a) * LANES, (first + a + 1) * LANES)
-                    wide = jnp.broadcast_to(piece[a : a + 1], (hi_count, LANES)).astype(jnp.bfloat16)
-                    spread[base : base + hi_count, cols] = wide * highhot[:, cols]
-        cols = slice(first * LANES, (first + count) * LANES)
-        return lax.dot_general(
-            spread[:, cols], onehot[:, cols], (((1,), (1,)), ((), ())), preferred_element_type=jnp.float32
-        )
-
-    placed_v[...] = place(gbar_v, 1.0, store_rows, gen_rows)
+                    row = jnp.broadcast_to(piece[a : a + 1], (hi_count, LANES)).astype(jnp.bfloat16)
+                    spread[first + a, base : base + hi_count] = row * highhot[first + a]
+        jobs = []
+        for t in range(count // 4):
+            a = first + 4 * t
+            left = jnp.concatenate([wide(spread, a, 2), wide(spread, a + 2, 2)], axis=0)
+            right = jnp.concatenate([wide(onehot, a, 2), wide(onehot, a + 2, 2)], axis=0)
+            jobs.append((t % 2, left, right))
+        height = rows * SPLITS * hi_count
+
+        def finish(accs):
+            multiply([(i, accs[i][0], left, right) for i, left, right in jobs], True)
+            for i in range(2):
+                both = pltpu.matmul_pop(accs[i][0])
+                part = both[:height, :LANES] + both[height:, LANES:]
+                target[...] = part + (start if i == 0 else target[...])
+
+        scoped(2 * height, 1, finish)
+
+    place(gbar_v, 1.0, store_rows, gen_rows, 0.0, placed_v)
 
     arrive(cross_r.at[0], recv_sem.at[5])
     hour_upper = total_v[...]
@@ -265,7 +311,8 @@
         def _(j=j):
             above_copy(j).start()
     total_v[...] = total_v[...] + above
-    placed = placed_v[...] + place(sbar_v, -1.0, 0, store_rows)
+    place(sbar_v, -1.0, 0, store_rows, placed_v[...], placed_v)
+    placed = placed_v[...]
     for r in range(rows):
         total = None
         for p in range(SPLITS):
@@ -285,10 +332,19 @@
         balance_o[:, r : r + 1] = balance_v[:, r : r + 1] + SIGMA * node_scale * jnp.sum(inject, keepdims=True)
         for j in range(hi_count):
             inj8[r : r + 1, j * LANES : (j + 1) * LANES] = inject[j : j + 1]
-    line_flows = lax.dot_general(
-        inj8[...].astype(jnp.bfloat16), ptdf_v[...], (((1,), (1,)), ((), ())),
-        preferred_element_type=jnp.float32,
-    )
+    inject_half = inj8[...].astype(jnp.bfloat16)
+    for first in range(0, line_tiles, THIN):
+        def lines_group(accs, first=first):
+            group = range(first, min(first + THIN, line_tiles))
+            multiply([
+                (k % 2, accs[k % 2][n - first], inject_half[:, cols(k)], tile(k, n))
+                for n in group for k in range(node_tiles)
+            ], True)
+            for i, n in enumerate(group):
+                line8[:, cols(n)] = pltpu.matmul_pop(accs[0][i]) + pltpu.matmul_pop(accs[1][i])
+
+        scoped(padded, THIN, lines_group)
+    line_flows = line8[...]
     shifted = flow8[...] + SIGMA * line_flows
     limit = limit1[...]
     line_next = shifted - SIGMA * jnp.minimum(jnp.maximum(shifted * (1.0 / SIGMA), -limit), limit)
@@ -349,6 +405,7 @@
 
 
 def local(
+    mesh,
     demand, avail, ptdf, line_limit, gen_cost, gen_cap, gen_node, store_node, store_power,
     capex, gen_state, store_state, level_upper, level_lower, flow_dual, balance_dual, capacity,
 ):
@@ -376,7 +433,7 @@
     f32 = jnp.float32
     gen_rows, store_rows = args[6].shape[0], args[7].shape[0]
     line_local, hi_count = ptdf.shape[0], nodes // LANES
-    padded = max(8, -(-rows // 8) * 8)
+    padded = max(16, -(-rows // 16) * 16)
     out_shapes = [
         (rows, gen_rows, LANES), (rows, store_rows, LANES), (store_rows, LANES),
         (rows, 1, line_local), (rows, store_rows, LANES), (rows, store_rows, LANES),
@@ -388,11 +445,13 @@
     block_rows = store_rows * jnp.dtype(LINK).itemsize // 4
     sent_rows = 2 * rows * hi_count + (hours - 1) * (years_dev + 1) * block_rows + (hours + 1) * years * block_rows
     scratch = [pltpu.VMEM(a.shape, a.dtype) for a in args]
+    scratch[2] = pltpu.VMEM((hi_count, line_local, LANES), ptdf.dtype)
     scratch += [
         pltpu.VMEM((padded, line_local), f32), pltpu.VMEM((1, line_local), f32),
         pltpu.VMEM((rows, nodes), f32), pltpu.VMEM((rows, nodes), f32),
         pltpu.VMEM((rows, hi_count, LANES), f32), pltpu.VMEM((rows, hi_count, LANES), f32),
-        pltpu.VMEM((padded, nodes), f32), pltpu.VMEM((rows, gen_rows, LANES), f32),
+        pltpu.VMEM((padded, nodes), f32), pltpu.VMEM((padded, line_local), f32),
+        pltpu.VMEM((rows, gen_rows, LANES), f32),
         pltpu.VMEM((rows, hi_count, LANES), f32),
         pltpu.VMEM(blocks, LINK), pltpu.VMEM((h1,) + blocks, LINK),
         pltpu.VMEM(block, f32), pltpu.VMEM((hours, y1) + block, LINK),
@@ -400,9 +459,9 @@
         pltpu.VMEM(blocks, LINK), pltpu.VMEM((h1,) + blocks, LINK),
         pltpu.VMEM((rows, gen_rows, LANES), f32), pltpu.VMEM((rows, store_rows, LANES), f32),
         pltpu.VMEM((rows, store_rows, LANES), f32),
-        pltpu.VMEM((rows * SPLITS * hi_count, (gen_rows + store_rows) * LANES), jnp.bfloat16),
-        pltpu.VMEM((LANES, (gen_rows + store_rows) * LANES), jnp.bfloat16),
-        pltpu.VMEM((hi_count, (gen_rows + store_rows) * LANES), jnp.bfloat16),
+        pltpu.VMEM((gen_rows + store_rows, rows * SPLITS * hi_count, LANES), jnp.bfloat16),
+        pltpu.VMEM((gen_rows + store_rows, LANES, LANES), jnp.bfloat16),
+        pltpu.VMEM((gen_rows + store_rows, hi_count, LANES), jnp.bfloat16),
         pltpu.VMEM((rows * SPLITS * hi_count, LANES), f32),
         pltpu.VMEM((sent_rows, LANES), f32),
         dma((3,)), dma, dma((7,)), pltpu.SemaphoreType.REGULAR,
@@ -439,4 +498,10 @@
         line, line, row, row, row, row, row, P(("groups", "years"), "hours"), P(("groups", "lines")),
     )
     out_specs = (row, row, P(("groups", "lines")), P(("groups", "years"), "hours"), row, row, row)
-    return jax.shard_map(local, mesh=mesh, in_specs=in_specs, out_specs=out_specs, check_vma=False)
+    step = jax.shard_map(functools.partial(local, mesh), mesh=mesh, in_specs=in_specs, out_specs=out_specs, check_vma=False)
+
+    def run(*args):
+        with jax.sharding.use_abstract_mesh(mesh.abstract_mesh):
+            return step(*args)
+
+    return run

time: 12.1 us -> 11.4 us (0.942)
  Pallas kernels: 11.3 us -> 10.6 us
    pallas_call x1, Pallas kernels: 10.6 us -> 9.97 us  [local(): pl.pallas_call(functools.partial(step_kernel, sizes), out_shape=[pltpu.VM...]
where the time goes in v3:
time: 11.4 us; the launch traced here: 11.3 us
  Pallas kernels  10.6 us (93%)
  between operations  0.65 us (6%)
    pallas_call x1, Pallas kernels, local(): pl.pallas_call(functools.partial(step_kernel, sizes), out_shape=[pltpu.VM...  9.97 us
    pallas_call x1, Pallas kernels, local(): pl.pallas_call(functools.partial(finish_kernel, len(results)), out_shape=...  0.66 us

profile of v3, /device:TPU:1, one launch (start us, length us, event | category | flops | bytes accessed | tf_op | source)
XLA Modules:
  0.0 11.3 jit_solution(6571759033056837714)
XLA Ops:
  0.6 10.0 %shard_map.216 = (f32[2,16,128]{2,1,0:T(8,128)S(1)}, f32[2,32,128]{2,1,0:T(8,128)S(1)}, f32[32,128]{1,0:T(8,128)S(1)}, f32[2,1,768]{2,1,0:T(1,128)S(1)}, f32[2,3...) custom-call(bf16[2,2048]{1,0:T(2,128)(2,1)} %bitcast.29, bf16[2,2048]{1,0:T(2,128)(2,1)} %bitcast.30, ...), custom_call_target="tpu_custom_call" | custom-call | tf_op jit(solution)/shard_map/pallas_call | solution.py:469
  10.6 0.7 %shard_map.217 = (f32[2,16,128]{2,1,0:T(8,128)}, f32[2,32,128]{2,1,0:T(8,128)}, f32[32,128]{1,0:T(8,128)}, f32[2,1,768]{2,1,0:T(1,128)}, f32[2,32,128]{2,1,0:T(8...) custom-call(f32[2,16,128]{2,1,0:T(8,128)S(1)} %get-tuple-element.21.refs_0_, f32[2,32,128]{2,1,0:T(8,128)S(1)} %get-tuple-element.22.refs_1_, ...), custom_call_target="tpu_custom_call" | custom-call | tf_op jit(solution)/shard_map/pallas_call | solution.py:479

commit v4 on v3

--- a/solution.py
+++ b/solution.py
@@ -27,9 +27,10 @@
     demand_v, avail_v, ptdf_v, limit_v, cost_v, cap_v, gnode_v, snode_v, power_v,
     capex_v, gen_v, store_v, upper_v, lower_v, flow_v, capacity_v, balance_v,
     flow8, limit1, net_s, net_r, inj_s, inj_r, inj8, line8, avail_d, demand_d,
-    dual_s, dual_r, total_v, cross_r, above_s, above_r, bar_s, bar_r,
-    gbar_v, sbar_v, price_v, spread, onehot, highhot, placed_v, sent,
-    in_sem, send_sem, recv_sem, year_ready,
+    dual_s, dual_r, total_v, cross_r, above_s, above_r, up_s, up_r, bar_s, bar_r,
+    gbar_v, sbar_v, price_v, onehot, highhot, placed_v, sent,
+    mate_s, mate_v, mate_node, mate_bar, mate_r, bal_s, bal_r,
+    in_sem, send_sem, recv_sem, year_ready, hour_ready,
 ):
     years_dev, hours_dev, hours, years, level_scale, node_scale, hour_count = sizes
     rows = years_dev * hours_dev
@@ -39,7 +40,7 @@
     gen_rows, store_rows = gnode_v.shape[0], snode_v.shape[0]
     link = dual_s.dtype
     block_rows = store_rows * link.itemsize // 4
-    base_rows = 2 * rows * hi_count + ((hours - 1) * (years_dev + 1) + years - 1) * block_rows
+    base_rows = 2 * rows * hi_count + 8 * rows + ((hours - 1) * (years_dev + 1) + years - 1) * block_rows
 
     order = (
         (upper_h, upper_v, 0), (lower_h, lower_v, 0), (flow_h, flow_v, 1),
@@ -87,13 +88,18 @@
 
     dual_r[...] = jnp.zeros_like(dual_r)
     bar_r[...] = jnp.zeros_like(bar_r)
+    up_r[...] = jnp.zeros_like(up_r)
     cross_r[...] = jnp.zeros_like(cross_r)
+    mate_r[...] = jnp.zeros_like(mate_r)
     above_r[...] = jnp.zeros_like(above_r)
     ready(partner)
     for k in range(1, hours):
         @pl.when(me_h + k < hours)
         def _(k=k):
             ready(peer(k, 0))
+        @pl.when(jnp.logical_and(me_h + k < hours, me_l == 1))
+        def _(k=k):
+            ready({**peer(k, 0), **partner})
     for j in range(1, years):
         @pl.when(me_y + j < years)
         def _(j=j):
@@ -103,11 +109,15 @@
                 def _(k=k):
                     ready(peer(k, j))
 
-    pl.semaphore_wait(barrier, 1 + me_y + me_h * (1 + me_y))
+    pl.semaphore_wait(barrier, 1 + me_y + me_h * (2 + me_y - me_l))
     for j in range(1, years):
         @pl.when(me_y + j >= years)
         def _(j=j):
             pl.semaphore_signal(year_ready, inc=1, device_id=peer(0, j), device_id_type=MESH)
+    for k in range(hours - 1, 0, -1):
+        @pl.when(me_h >= k)
+        def _(k=k):
+            pl.semaphore_signal(hour_ready, inc=1, device_id=peer(hours - k, 0), device_id_type=MESH)
 
     loads[0].wait()
     loads[1].wait()
@@ -138,6 +148,16 @@
     def bar_copy(k):
         return remote(bar_s, bar_r.at[k - 1], 3, peer(k, 0))
 
+    def mate_dual_copy(k):
+        return remote(dual_s.at[pl.ds(0, years_dev)], mate_r.at[k - 1], 8, {**peer(hours - k, 0), **partner})
+
+    node_copy = remote(snode_v, mate_node, 9, partner)
+    mate_copy = remote(mate_s, mate_v, 10, partner)
+    bal_copy = remote(bal_s, bal_r, 11, partner)
+
+    def up_copy(k):
+        return remote(up_s, up_r.at[k - 1], 7, peer(k, 0))
+
     def cross_copy(k, j):
         slot = cross_r.at[k, j - 1]
         return remote(dual_s.at[years_dev], slot, 4 if k else 5, peer(hours - k, years - j))
@@ -148,19 +168,23 @@
     net_copy = remote(net_s, net_r, 0, partner)
     inj_copy = remote(inj_s, inj_r, 1, partner)
 
+    for j in range(1, years):
+        for k in range(hours - 1, 0, -1):
+            @pl.when(jnp.logical_and(me_h >= k, me_y >= j))
+            def _(k=k, j=j):
+                cross_copy(k, j).start()
     for k in range(hours - 1, 0, -1):
         @pl.when(me_h >= k)
         def _(k=k):
             dual_copy(k).start()
+
+        @pl.when(jnp.logical_and(me_h >= k, me_l == 0))
+        def _(k=k):
+            mate_dual_copy(k).start()
     for j in range(1, years):
         @pl.when(me_y >= j)
         def _(j=j):
             cross_copy(0, j).start()
-    for j in range(1, years):
-        for k in range(hours - 1, 0, -1):
-            @pl.when(jnp.logical_and(me_h >= k, me_y >= j))
-            def _(k=k, j=j):
-                cross_copy(k, j).start()
 
     for copy in loads[2 : 3 + hi_count]:
         copy.wait()
@@ -193,20 +217,23 @@
 
     for copy in loads[3 + hi_count :]:
         copy.wait()
+
+    @pl.when(me_l == 0)
+    def _():
+        node_copy.start()
     high_rows = lax.broadcasted_iota(jnp.int32, (hi_count, LANES), 0)
     lane_rows = lax.broadcasted_iota(jnp.int32, (LANES, LANES), 0)
 
-    def node_row(a):
-        if a < store_rows:
-            return snode_v[a : a + 1, :]
-        return gnode_v[a - store_rows : a - store_rows + 1, :]
-
-    for a in range(store_rows + gen_rows):
-        low = jnp.broadcast_to(node_row(a) % LANES, (LANES, LANES))
-        onehot[a] = jnp.where(low == lane_rows, 1.0, 0.0).astype(jnp.bfloat16)
-        high = jnp.broadcast_to(node_row(a) // LANES, (hi_count, LANES))
-        highhot[a] = jnp.where(high == high_rows, 1.0, 0.0).astype(jnp.bfloat16)
-
+    def encode(ref, first, count):
+        for a in range(count):
+            row = ref[a : a + 1, :]
+            low = jnp.broadcast_to(row % LANES, (LANES, LANES))
+            onehot[first + a] = jnp.where(low == lane_rows, 1.0, 0.0).astype(jnp.bfloat16)
+            high = jnp.broadcast_to(row // LANES, (hi_count, LANES))
+            highhot[first + a] = jnp.where(high == high_rows, 1.0, 0.0).astype(jnp.bfloat16)
+
+    encode(snode_v, 0, store_rows)
+    encode(gnode_v, store_rows, gen_rows)
     for r in range(rows):
         for j in range(hi_count):
             piece = slice(j * LANES, (j + 1) * LANES)
@@ -232,6 +259,19 @@
         for b in range(0, store_rows, 8):
             price_v[r, b : b + 8] = gather(r, snode_v[b : b + 8])
 
+    @pl.when(me_l == 0)
+    def _():
+        mate_s[2 * rows] = power_v[...]
+        for y in range(years_dev):
+            own = None
+            for h in reversed(range(hours_dev)):
+                r = y * hours_dev + h
+                diff = upper_v[r] - lower_v[r]
+                own = diff if own is None else own + diff
+                mate_s[r] = store_v[r] - TAU * (level_scale * own - price_v[r])
+                mate_s[rows + r] = store_v[r]
+        mate_copy.start()
+
     for r in range(rows):
         for b in range(0, gen_rows, 8):
             part = slice(b, b + 8)
@@ -242,20 +282,27 @@
             gbar_v[r, part] = 2.0 * new - gen_v[r, part]
 
     def place(values, sign, first, count, start, target):
+        pieces = []
         for r in range(rows):
             rest = sign * values[r]
-            for p in range(SPLITS):
+            for _ in range(SPLITS):
                 piece = rest.astype(jnp.bfloat16).astype(jnp.float32)
                 rest = rest - piece
-                base = (r * SPLITS + p) * hi_count
-                for a in range(count):
-                    row = jnp.broadcast_to(piece[a : a + 1], (hi_count, LANES)).astype(jnp.bfloat16)
-                    spread[first + a, base : base + hi_count] = row * highhot[first + a]
+                pieces.append(piece)
+
+        def spread(a):
+            return jnp.concatenate([
+                jnp.broadcast_to(piece[a : a + 1], (hi_count, LANES)).astype(jnp.bfloat16) * highhot[first + a]
+                for piece in pieces
+            ], axis=0)
+
+        def pair(make, a):
+            return jnp.concatenate([make(a), make(a + 1)], axis=1)
+
         jobs = []
         for t in range(count // 4):
-            a = first + 4 * t
-            left = jnp.concatenate([wide(spread, a, 2), wide(spread, a + 2, 2)], axis=0)
-            right = jnp.concatenate([wide(onehot, a, 2), wide(onehot, a + 2, 2)], axis=0)
+            left = jnp.concatenate([pair(spread, 4 * t), pair(spread, 4 * t + 2)], axis=0)
+            right = jnp.concatenate([wide(onehot, first + 4 * t, 2), wide(onehot, first + 4 * t + 2, 2)], axis=0)
             jobs.append((t % 2, left, right))
         height = rows * SPLITS * hi_count
 
@@ -270,12 +317,40 @@
 
     place(gbar_v, 1.0, store_rows, gen_rows, 0.0, placed_v)
 
+    def inject_part(r):
+        total = None
+        for p in range(SPLITS):
+            base = (r * SPLITS + p) * hi_count
+            piece = placed_v[base : base + hi_count]
+            total = piece if total is None else total + piece
+        return total
+
+    @pl.when(me_l == 0)
+    def _():
+        for r in range(rows):
+            inj_s[r] = inject_part(r)
+        inj_copy.start()
+
+    @pl.when(me_l == 1)
+    def _():
+        arrive(mate_node, recv_sem.at[9])
+        encode(mate_node, store_rows + gen_rows, store_rows)
+        arrive(mate_v, recv_sem.at[10])
+
     arrive(cross_r.at[0], recv_sem.at[5])
     hour_upper = total_v[...]
     for j in range(1, years):
         hour_upper = hour_upper + cross_r[0, j - 1].astype(jnp.float32)
     total_v[...] = hour_upper
-    bar_s[years_dev] = hour_upper.astype(link)
+    up_s[...] = hour_upper.astype(link)
+
+    @pl.when(me_h < hours - 1)
+    def _():
+        pl.semaphore_wait(hour_ready, hours - 1 - me_h)
+        for k in range(hours - 1, 0, -1):
+            @pl.when(me_h + k < hours)
+            def _(k=k):
+                up_copy(k).start()
 
     for count in range(1, hours):
         @pl.when(me_h + count == hours - 1)
@@ -312,24 +387,47 @@
             above_copy(j).start()
     total_v[...] = total_v[...] + above
     place(sbar_v, -1.0, 0, store_rows, placed_v[...], placed_v)
-    placed = placed_v[...]
-    for r in range(rows):
-        total = None
-        for p in range(SPLITS):
-            base = (r * SPLITS + p) * hi_count
-            piece = placed[base : base + hi_count]
-            total = piece if total is None else total + piece
-        inj_s[r] = total
-    inj_copy.start()
+
+    @pl.when(me_l == 1)
+    def _():
+        for r in range(rows):
+            inj_s[r] = inject_part(r)
+        inj_copy.start()
+
+    for r in range(rows):
+        part = None
+        for b in range(0, gen_rows, 8):
+            part = gbar_v[r, b : b + 8] if part is None else part + gbar_v[r, b : b + 8]
+        for b in range(0, store_rows, 8):
+            part = part - sbar_v[r, b : b + 8]
+        bal_s[r] = part
+    bal_copy.start()
 
     for c in range(line_local // LANES):
         limit1[:, c * LANES : (c + 1) * LANES] = limit_v[c : c + 1, :]
     inj8[...] = jnp.zeros_like(inj8)
 
+    @pl.when(me_l == 1)
+    def _():
+        for count in range(1, hours):
+            @pl.when(me_h + count == hours - 1)
+            def _(count=count):
+                arrive(mate_r.at[pl.ds(0, count)], recv_sem.at[8])
+        power = mate_v[2 * rows]
+        for y in range(years_dev):
+            beyond = mate_r[0, y].astype(jnp.float32)
+            for k in range(2, hours):
+                beyond = beyond + mate_r[k - 1, y].astype(jnp.float32)
+            for h in range(hours_dev):
+                r = y * hours_dev + h
+                new = mate_v[r] - TAU * level_scale * beyond
+                new = jnp.minimum(jnp.maximum(new, -power), power)
+                mate_bar[r] = 2.0 * new - mate_v[rows + r]
+        place(mate_bar, -1.0, store_rows + gen_rows, store_rows, placed_v[...], placed_v)
+
     inj_copy.wait_recv()
     for r in range(rows):
-        inject = inj_s[r] + inj_r[r] - demand_d[r]
-        balance_o[:, r : r + 1] = balance_v[:, r : r + 1] + SIGMA * node_scale * jnp.sum(inject, keepdims=True)
+        inject = inject_part(r) + inj_r[r] - demand_d[r]
         for j in range(hi_count):
             inj8[r : r + 1, j * LANES : (j + 1) * LANES] = inject[j : j + 1]
     inject_half = inj8[...].astype(jnp.bfloat16)
@@ -364,9 +462,10 @@
         @pl.when(me_h == count)
         def _(count=count):
             arrive(bar_r.at[pl.ds(0, count)], recv_sem.at[3])
+            arrive(up_r.at[pl.ds(0, count)], recv_sem.at[7])
     upper_total = total_v[...]
     for k in range(1, hours):
-        upper_total = upper_total + bar_r[k - 1, years_dev].astype(jnp.float32)
+        upper_total = upper_total + up_r[k - 1].astype(jnp.float32)
         for j in range(1, years):
             upper_total = upper_total + cross_r[k, j - 1].astype(jnp.float32)
     for j in range(1, years):
@@ -386,13 +485,25 @@
             upper_w[r] = jnp.maximum(upper_v[r] + SIGMA * (level - capacity_bar), 0.0)
             lower_w[r] = jnp.maximum(lower_v[r] - SIGMA * level, 0.0)
 
+    bal_copy.wait_recv()
+    for r in range(rows):
+        part = bal_s[r] + bal_r[r]
+        for b in range(0, hi_count, 8):
+            part = part - demand_d[r, b : b + 8]
+        balance_o[:, r : r + 1] = balance_v[:, r : r + 1] + SIGMA * node_scale * jnp.sum(part, keepdims=True)
+
     for y in range(years):
         for h in range(hours):
             blocks = h * y + (years - 1 - y if h < hours - 1 else 0)
-
-            @pl.when(jnp.logical_and(me_h == h, me_y == y))
-            def _(blocks=blocks):
-                arrive(sent.at[pl.ds(0, base_rows + blocks * block_rows)], send_sem)
+            extra = (2 * rows + 2) * store_rows + h * years_dev * block_rows
+
+            @pl.when(jnp.logical_and(jnp.logical_and(me_h == h, me_y == y), me_l == 0))
+            def _(size=base_rows + blocks * block_rows + extra):
+                arrive(sent.at[pl.ds(0, size)], send_sem)
+
+            @pl.when(jnp.logical_and(jnp.logical_and(me_h == h, me_y == y), me_l == 1))
+            def _(size=base_rows + blocks * block_rows):
+                arrive(sent.at[pl.ds(0, size)], send_sem)
 
 
 def finish_kernel(count, *refs):
@@ -443,7 +554,7 @@
     h1, y1 = max(hours - 1, 1), max(years - 1, 1)
     dma = pltpu.SemaphoreType.DMA
     block_rows = store_rows * jnp.dtype(LINK).itemsize // 4
-    sent_rows = 2 * rows * hi_count + (hours - 1) * (years_dev + 1) * block_rows + (hours + 1) * years * block_rows
+    sent_rows = 2 * rows * hi_count + 8 * rows + (2 * rows + 2) * store_rows + hours * years_dev * block_rows + (hours - 1) * (years_dev + 1) * block_rows + (hours + 1) * years * block_rows
     scratch = [pltpu.VMEM(a.shape, a.dtype) for a in args]
     scratch[2] = pltpu.VMEM((hi_count, line_local, LANES), ptdf.dtype)
     scratch += [
@@ -456,15 +567,18 @@
         pltpu.VMEM(blocks, LINK), pltpu.VMEM((h1,) + blocks, LINK),
         pltpu.VMEM(block, f32), pltpu.VMEM((hours, y1) + block, LINK),
         pltpu.VMEM(block, LINK), pltpu.VMEM((y1,) + block, LINK),
-        pltpu.VMEM(blocks, LINK), pltpu.VMEM((h1,) + blocks, LINK),
+        pltpu.VMEM(block, LINK), pltpu.VMEM((h1,) + block, LINK),
+        pltpu.VMEM((years_dev,) + block, LINK), pltpu.VMEM((h1, years_dev) + block, LINK),
         pltpu.VMEM((rows, gen_rows, LANES), f32), pltpu.VMEM((rows, store_rows, LANES), f32),
         pltpu.VMEM((rows, store_rows, LANES), f32),
-        pltpu.VMEM((gen_rows + store_rows, rows * SPLITS * hi_count, LANES), jnp.bfloat16),
-        pltpu.VMEM((gen_rows + store_rows, LANES, LANES), jnp.bfloat16),
-        pltpu.VMEM((gen_rows + store_rows, hi_count, LANES), jnp.bfloat16),
+        pltpu.VMEM((gen_rows + 2 * store_rows, LANES, LANES), jnp.bfloat16),
+        pltpu.VMEM((gen_rows + 2 * store_rows, hi_count, LANES), jnp.bfloat16),
         pltpu.VMEM((rows * SPLITS * hi_count, LANES), f32),
         pltpu.VMEM((sent_rows, LANES), f32),
-        dma((3,)), dma, dma((7,)), pltpu.SemaphoreType.REGULAR,
+        pltpu.VMEM((2 * rows + 1,) + block, f32), pltpu.VMEM((2 * rows + 1,) + block, f32),
+        pltpu.VMEM(block, jnp.int32), pltpu.VMEM((rows,) + block, f32), pltpu.VMEM((h1, years_dev) + block, LINK),
+        pltpu.VMEM((rows, 8, LANES), f32), pltpu.VMEM((rows, 8, LANES), f32),
+        dma((3,)), dma, dma((12,)), pltpu.SemaphoreType.REGULAR, pltpu.SemaphoreType.REGULAR,
     ]
     results = pl.pallas_call(
         functools.partial(step_kernel, sizes),

time: 11.4 us -> 11.1 us (0.974)
  the two profiles are of different devices: /device:TPU:1 before, /device:TPU:0 now
where the time goes in v4:
time: 11.1 us; the launch traced here: 10.9 us
  Pallas kernels  10.3 us (93%)
  between operations  0.65 us (6%)
    pallas_call x1, Pallas kernels, local(): pl.pallas_call(functools.partial(step_kernel, sizes), out_shape=[pltpu.VM...  9.6 us
    pallas_call x1, Pallas kernels, local(): pl.pallas_call(functools.partial(finish_kernel, len(results)), out_shape=...  0.66 us

profile of v4, /device:TPU:0, one launch (start us, length us, event | category | flops | bytes accessed | tf_op | source)
XLA Modules:
  0.0 10.9 jit_solution(12596542343518095861)
XLA Ops:
  0.6 9.6 %shard_map.216 = (f32[2,16,128]{2,1,0:T(8,128)S(1)}, f32[2,32,128]{2,1,0:T(8,128)S(1)}, f32[32,128]{1,0:T(8,128)S(1)}, f32[2,1,768]{2,1,0:T(1,128)S(1)}, f32[2,3...) custom-call(bf16[2,2048]{1,0:T(2,128)(2,1)} %bitcast.29, bf16[2,2048]{1,0:T(2,128)(2,1)} %bitcast.30, ...), custom_call_target="tpu_custom_call" | custom-call | tf_op jit(solution)/shard_map/pallas_call | solution.py:583
  10.2 0.7 %shard_map.217 = (f32[2,16,128]{2,1,0:T(8,128)}, f32[2,32,128]{2,1,0:T(8,128)}, f32[32,128]{1,0:T(8,128)}, f32[2,1,768]{2,1,0:T(1,128)}, f32[2,32,128]{2,1,0:T(8...) custom-call(f32[2,16,128]{2,1,0:T(8,128)S(1)} %get-tuple-element.21.refs_0_, f32[2,32,128]{2,1,0:T(8,128)S(1)} %get-tuple-element.22.refs_1_, ...), custom_call_target="tpu_custom_call" | custom-call | tf_op jit(solution)/shard_map/pallas_call | solution.py:593

commit v5 on v4

--- a/solution.py
+++ b/solution.py
@@ -29,7 +29,7 @@
     flow8, limit1, net_s, net_r, inj_s, inj_r, inj8, line8, avail_d, demand_d,
     dual_s, dual_r, total_v, cross_r, above_s, above_r, up_s, up_r, bar_s, bar_r,
     gbar_v, sbar_v, price_v, onehot, highhot, placed_v, sent,
-    mate_s, mate_v, mate_node, mate_bar, mate_r, bal_s, bal_r,
+    mate_s, mate_v, mate_node, mate_bar, mate_sum, mate_r, bal_s, bal_r,
     in_sem, send_sem, recv_sem, year_ready, hour_ready,
 ):
     years_dev, hours_dev, hours, years, level_scale, node_scale, hour_count = sizes
@@ -40,15 +40,15 @@
     gen_rows, store_rows = gnode_v.shape[0], snode_v.shape[0]
     link = dual_s.dtype
     block_rows = store_rows * link.itemsize // 4
-    base_rows = 2 * rows * hi_count + 8 * rows + ((hours - 1) * (years_dev + 1) + years - 1) * block_rows
+    base_rows = 2 * rows * hi_count + 8 * rows + (hours - 1 + years - 1) * block_rows
 
     order = (
         (upper_h, upper_v, 0), (lower_h, lower_v, 0), (flow_h, flow_v, 1),
     ) + tuple((ptdf_h.at[:, pl.ds(j * LANES, LANES)], ptdf_v.at[j], 1) for j in range(hi_count)) + (
-        (snode_h, snode_v, 2), (gnode_h, gnode_v, 2), (store_h, store_v, 2), (power_h, power_v, 2),
-        (gen_h, gen_v, 2), (cost_h, cost_v, 2), (cap_h, cap_v, 2), (avail_h, avail_v, 2),
-        (demand_h, demand_v, 2), (limit_h, limit_v, 2), (capex_h, capex_v, 2), (capacity_h, capacity_v, 2),
-        (balance_h, balance_v, 2),
+        (snode_h, snode_v, 1), (gnode_h, gnode_v, 1), (store_h, store_v, 1), (power_h, power_v, 1),
+        (gen_h, gen_v, 1), (cost_h, cost_v, 1), (cap_h, cap_v, 1), (avail_h, avail_v, 1),
+        (demand_h, demand_v, 1), (limit_h, limit_v, 1), (capex_h, capex_v, 1), (capacity_h, capacity_v, 1),
+        (balance_h, balance_v, 1),
     )
     loads = [pltpu.make_async_copy(s, d, in_sem.at[i]) for s, d, i in order]
     for copy in loads:
@@ -148,22 +148,25 @@
     def bar_copy(k):
         return remote(bar_s, bar_r.at[k - 1], 3, peer(k, 0))
 
+    def mate_bar_copy(k):
+        return remote(mate_sum, bar_r.at[k - 1], 3, {**peer(k, 0), **partner})
+
     def mate_dual_copy(k):
-        return remote(dual_s.at[pl.ds(0, years_dev)], mate_r.at[k - 1], 8, {**peer(hours - k, 0), **partner})
-
-    node_copy = remote(snode_v, mate_node, 9, partner)
-    mate_copy = remote(mate_s, mate_v, 10, partner)
-    bal_copy = remote(bal_s, bal_r, 11, partner)
+        return remote(dual_s.at[pl.ds(0, years_dev)], mate_r.at[k - 1], 6, {**peer(hours - k, 0), **partner})
+
+    node_copy = remote(snode_v, mate_node, 4, partner)
+    mate_copy = remote(mate_s, mate_v, 4, partner)
+    bal_copy = remote(bal_s, bal_r, 7, partner)
 
     def up_copy(k):
-        return remote(up_s, up_r.at[k - 1], 7, peer(k, 0))
+        return remote(up_s, up_r.at[k - 1], 3, peer(k, 0))
 
     def cross_copy(k, j):
         slot = cross_r.at[k, j - 1]
-        return remote(dual_s.at[years_dev], slot, 4 if k else 5, peer(hours - k, years - j))
+        return remote(dual_s.at[years_dev], slot, 3 if k else 5, peer(hours - k, years - j))
 
     def above_copy(j):
-        return remote(above_s, above_r.at[j - 1], 6, peer(0, j))
+        return remote(above_s, above_r.at[j - 1], 3, peer(0, j))
 
     net_copy = remote(net_s, net_r, 0, partner)
     inj_copy = remote(inj_s, inj_r, 1, partner)
@@ -186,7 +189,7 @@
         def _(j=j):
             cross_copy(0, j).start()
 
-    for copy in loads[2 : 3 + hi_count]:
+    for copy in loads[2:]:
         copy.wait()
     flow8[...] = jnp.zeros_like(flow8)
     for r in range(rows):
@@ -215,9 +218,6 @@
         def _(j=j):
             cross_copy(0, years - j).start()
 
-    for copy in loads[3 + hi_count :]:
-        copy.wait()
-
     @pl.when(me_l == 0)
     def _():
         node_copy.start()
@@ -333,9 +333,8 @@
 
     @pl.when(me_l == 1)
     def _():
-        arrive(mate_node, recv_sem.at[9])
+        arrive(sent.at[pl.ds(0, (2 * rows + 2) * store_rows)], recv_sem.at[4])
         encode(mate_node, store_rows + gen_rows, store_rows)
-        arrive(mate_v, recv_sem.at[10])
 
     arrive(cross_r.at[0], recv_sem.at[5])
     hour_upper = total_v[...]
@@ -378,7 +377,7 @@
             bar_total = sbar if bar_total is None else bar_total + sbar
         bar_s[y] = bar_total.astype(link)
     for k in range(hours - 1, 0, -1):
-        @pl.when(me_h + k < hours)
+        @pl.when(jnp.logical_or(me_h + k == hours - 1, jnp.logical_and(me_h + k < hours, me_l == 1)))
         def _(k=k):
             bar_copy(k).start()
     for j in range(1, years):
@@ -412,17 +411,25 @@
         for count in range(1, hours):
             @pl.when(me_h + count == hours - 1)
             def _(count=count):
-                arrive(mate_r.at[pl.ds(0, count)], recv_sem.at[8])
+                arrive(mate_r.at[pl.ds(0, count)], recv_sem.at[6])
         power = mate_v[2 * rows]
         for y in range(years_dev):
             beyond = mate_r[0, y].astype(jnp.float32)
             for k in range(2, hours):
                 beyond = beyond + mate_r[k - 1, y].astype(jnp.float32)
+            bar_total = None
             for h in range(hours_dev):
                 r = y * hours_dev + h
                 new = mate_v[r] - TAU * level_scale * beyond
                 new = jnp.minimum(jnp.maximum(new, -power), power)
-                mate_bar[r] = 2.0 * new - mate_v[rows + r]
+                sbar = 2.0 * new - mate_v[rows + r]
+                mate_bar[r] = sbar
+                bar_total = sbar if bar_total is None else bar_total + sbar
+            mate_sum[y] = bar_total.astype(link)
+        for k in range(hours - 2, 0, -1):
+            @pl.when(me_h + k < hours - 1)
+            def _(k=k):
+                mate_bar_copy(k).start()
         place(mate_bar, -1.0, store_rows + gen_rows, store_rows, placed_v[...], placed_v)
 
     inj_copy.wait_recv()
@@ -449,20 +456,20 @@
     for r in range(rows):
         flow_w[r] = line_next[r : r + 1]
 
-    for j in range(1, years):
-        for k in range(1, hours):
-            @pl.when(jnp.logical_and(me_h + k == hours - 1, me_y + j == years - 1))
-            def _(k=k, j=j):
-                arrive(cross_r.at[pl.ds(1, k), pl.ds(0, j)], recv_sem.at[4])
-
-        @pl.when(jnp.logical_and(me_h < hours - 1, me_y == j))
-        def _(j=j):
-            arrive(above_r.at[pl.ds(0, j)], recv_sem.at[6])
-    for count in range(1, hours):
-        @pl.when(me_h == count)
-        def _(count=count):
-            arrive(bar_r.at[pl.ds(0, count)], recv_sem.at[3])
-            arrive(up_r.at[pl.ds(0, count)], recv_sem.at[7])
+    for y in range(years):
+        for h in range(hours):
+            late = h * (years_dev + 1) + (hours - 1 - h) * (years - 1 - y) + (y if h < hours - 1 else 0)
+            if late:
+                @pl.when(jnp.logical_and(me_h == h, me_y == y))
+                def _(size=late * block_rows):
+                    arrive(sent.at[pl.ds(0, size)], recv_sem.at[3])
+    bal_copy.wait_recv()
+    for r in range(rows):
+        part = bal_s[r] + bal_r[r]
+        for b in range(0, hi_count, 8):
+            part = part - demand_d[r, b : b + 8]
+        balance_o[:, r : r + 1] = balance_v[:, r : r + 1] + SIGMA * node_scale * jnp.sum(part, keepdims=True)
+
     upper_total = total_v[...]
     for k in range(1, hours):
         upper_total = upper_total + up_r[k - 1].astype(jnp.float32)
@@ -485,24 +492,19 @@
             upper_w[r] = jnp.maximum(upper_v[r] + SIGMA * (level - capacity_bar), 0.0)
             lower_w[r] = jnp.maximum(lower_v[r] - SIGMA * level, 0.0)
 
-    bal_copy.wait_recv()
-    for r in range(rows):
-        part = bal_s[r] + bal_r[r]
-        for b in range(0, hi_count, 8):
-            part = part - demand_d[r, b : b + 8]
-        balance_o[:, r : r + 1] = balance_v[:, r : r + 1] + SIGMA * node_scale * jnp.sum(part, keepdims=True)
-
     for y in range(years):
         for h in range(hours):
-            blocks = h * y + (years - 1 - y if h < hours - 1 else 0)
-            extra = (2 * rows + 2) * store_rows + h * years_dev * block_rows
+            blocks = h * years_dev + h * y + (years - 1 - y if h < hours - 1 else 0)
+            near = years_dev * (h + (1 if h < hours - 1 else 0))
+            far = years_dev * (hours - 1 - h + max(hours - 2 - h, 0))
+            extra = (2 * rows + 2) * store_rows
 
             @pl.when(jnp.logical_and(jnp.logical_and(me_h == h, me_y == y), me_l == 0))
-            def _(size=base_rows + blocks * block_rows + extra):
+            def _(size=base_rows + (blocks + near) * block_rows + extra):
                 arrive(sent.at[pl.ds(0, size)], send_sem)
 
             @pl.when(jnp.logical_and(jnp.logical_and(me_h == h, me_y == y), me_l == 1))
-            def _(size=base_rows + blocks * block_rows):
+            def _(size=base_rows + (blocks + far) * block_rows):
                 arrive(sent.at[pl.ds(0, size)], send_sem)
 
 
@@ -554,7 +556,7 @@
     h1, y1 = max(hours - 1, 1), max(years - 1, 1)
     dma = pltpu.SemaphoreType.DMA
     block_rows = store_rows * jnp.dtype(LINK).itemsize // 4
-    sent_rows = 2 * rows * hi_count + 8 * rows + (2 * rows + 2) * store_rows + hours * years_dev * block_rows + (hours - 1) * (years_dev + 1) * block_rows + (hours + 1) * years * block_rows
+    sent_rows = 2 * rows * hi_count + 8 * rows + (2 * rows + 2) * store_rows + 2 * hours * years_dev * block_rows + (hours - 1) * (years_dev + 1) * block_rows + (hours + 1) * years * block_rows
     scratch = [pltpu.VMEM(a.shape, a.dtype) for a in args]
     scratch[2] = pltpu.VMEM((hi_count, line_local, LANES), ptdf.dtype)
     scratch += [
@@ -576,9 +578,10 @@
         pltpu.VMEM((rows * SPLITS * hi_count, LANES), f32),
         pltpu.VMEM((sent_rows, LANES), f32),
         pltpu.VMEM((2 * rows + 1,) + block, f32), pltpu.VMEM((2 * rows + 1,) + block, f32),
-        pltpu.VMEM(block, jnp.int32), pltpu.VMEM((rows,) + block, f32), pltpu.VMEM((h1, years_dev) + block, LINK),
+        pltpu.VMEM(block, jnp.int32), pltpu.VMEM((rows,) + block, f32), pltpu.VMEM((years_dev,) + block, LINK),
+        pltpu.VMEM((h1, years_dev) + block, LINK),
         pltpu.VMEM((rows, 8, LANES), f32), pltpu.VMEM((rows, 8, LANES), f32),
-        dma((3,)), dma, dma((12,)), pltpu.SemaphoreType.REGULAR, pltpu.SemaphoreType.REGULAR,
+        dma((2,)), dma, dma((8,)), pltpu.SemaphoreType.REGULAR, pltpu.SemaphoreType.REGULAR,
     ]
     results = pl.pallas_call(
         functools.partial(step_kernel, sizes),

time: 11.1 us -> 10.9 us (0.982)
  Pallas kernels: 10.3 us -> 10.1 us
    pallas_call x1, Pallas kernels: 9.6 us -> 9.43 us  [local(): pl.pallas_call(functools.partial(step_kernel, sizes), out_shape=[pltpu.VM...]
where the time goes in v5:
time: 10.9 us; the launch traced here: 10.7 us
  Pallas kernels  10.1 us (93%)
  between operations  0.65 us (6%)
    pallas_call x1, Pallas kernels, local(): pl.pallas_call(functools.partial(step_kernel, sizes), out_shape=[pltpu.VM...  9.43 us
    pallas_call x1, Pallas kernels, local(): pl.pallas_call(functools.partial(finish_kernel, len(results)), out_shape=...  0.66 us

profile of v5, /device:TPU:0, one launch (start us, length us, event | category | flops | bytes accessed | tf_op | source)
XLA Modules:
  0.0 10.7 jit_solution(11775101364390115830)
XLA Ops:
  0.6 9.4 %shard_map.216 = (f32[2,16,128]{2,1,0:T(8,128)S(1)}, f32[2,32,128]{2,1,0:T(8,128)S(1)}, f32[32,128]{1,0:T(8,128)S(1)}, f32[2,1,768]{2,1,0:T(1,128)S(1)}, f32[2,3...) custom-call(bf16[2,2048]{1,0:T(2,128)(2,1)} %bitcast.29, bf16[2,2048]{1,0:T(2,128)(2,1)} %bitcast.30, ...), custom_call_target="tpu_custom_call" | custom-call | tf_op jit(solution)/shard_map/pallas_call | solution.py:586
  10.1 0.7 %shard_map.217 = (f32[2,16,128]{2,1,0:T(8,128)}, f32[2,32,128]{2,1,0:T(8,128)}, f32[32,128]{1,0:T(8,128)}, f32[2,1,768]{2,1,0:T(1,128)}, f32[2,32,128]{2,1,0:T(8...) custom-call(f32[2,16,128]{2,1,0:T(8,128)S(1)} %get-tuple-element.21.refs_0_, f32[2,32,128]{2,1,0:T(8,128)S(1)} %get-tuple-element.22.refs_1_, ...), custom_call_target="tpu_custom_call" | custom-call | tf_op jit(solution)/shard_map/pallas_call | solution.py:596

commit v6 on v5

--- a/solution.py
+++ b/solution.py
@@ -15,6 +15,7 @@
 SPLITS = 2
 TILE = 256
 THIN = 4
+DEPTH = 1
 LINK = jnp.bfloat16
 MESH = pl.DeviceIdType.MESH
 
@@ -29,7 +30,7 @@
     flow8, limit1, net_s, net_r, inj_s, inj_r, inj8, line8, avail_d, demand_d,
     dual_s, dual_r, total_v, cross_r, above_s, above_r, up_s, up_r, bar_s, bar_r,
     gbar_v, sbar_v, price_v, onehot, highhot, placed_v, sent,
-    mate_s, mate_v, mate_node, mate_bar, mate_sum, mate_r, bal_s, bal_r,
+    mate_s, mate_v, mate_node, mate_bar, mate_sum, mate_r, bal_s, bal_r, ptdf_t,
     in_sem, send_sem, recv_sem, year_ready, hour_ready,
 ):
     years_dev, hours_dev, hours, years, level_scale, node_scale, hour_count = sizes
@@ -242,6 +243,25 @@
             piece = slice(j * LANES, (j + 1) * LANES)
             avail_d[r, j : j + 1, :] = avail_v[r : r + 1, piece].astype(jnp.float32)
 
+    diagonal = lax.broadcasted_iota(jnp.int32, (TILE, TILE), 0) == lax.broadcasted_iota(jnp.int32, (TILE, TILE), 1)
+    identity = jnp.where(diagonal, 1.0, 0.0).astype(jnp.bfloat16)
+
+    def turn(accs):
+        work = [(k, n) for k in range(node_tiles) for n in range(line_tiles)]
+        held = 2 * DEPTH
+        for i in range(len(work) + held):
+            if i >= held:
+                k, n = work[i - held]
+                turned = pltpu.matmul_pop(accs[i % 2][(i // 2) % DEPTH]).astype(ptdf_t.dtype)
+                for c in range(2):
+                    ptdf_t[k, n, c] = turned[:, c * LANES : (c + 1) * LANES]
+            if i < len(work):
+                k, n = work[i]
+                pltpu.matmul_push_rhs(tile(k, n), (i // 2) % 2, i % 2, transpose=True)
+                pltpu.matmul_acc_lhs(accs[i % 2][(i // 2) % DEPTH], identity, load_staged_rhs=(i // 2) % 2)
+
+    scoped(TILE, DEPTH, turn)
+
     net_copy.wait_recv()
     prices = net_s[...] + net_r[...]
 
@@ -317,6 +337,12 @@
 
     place(gbar_v, 1.0, store_rows, gen_rows, 0.0, placed_v)
 
+    for r in range(rows):
+        part = gbar_v[r, 0:8]
+        for b in range(8, gen_rows, 8):
+            part = part + gbar_v[r, b : b + 8]
+        bal_s[r] = part
+
     def inject_part(r):
         total = None
         for p in range(SPLITS):
@@ -331,10 +357,6 @@
             inj_s[r] = inject_part(r)
         inj_copy.start()
 
-    @pl.when(me_l == 1)
-    def _():
-        arrive(sent.at[pl.ds(0, (2 * rows + 2) * store_rows)], recv_sem.at[4])
-        encode(mate_node, store_rows + gen_rows, store_rows)
 
     arrive(cross_r.at[0], recv_sem.at[5])
     hour_upper = total_v[...]
@@ -359,6 +381,10 @@
     for k in range(2, hours):
         above = above + dual_r[k - 1, years_dev].astype(jnp.float32)
     above_s[...] = above.astype(link)
+    for j in range(1, years):
+        @pl.when(jnp.logical_and(me_h < hours - 1, me_y + j < years))
+        def _(j=j):
+            above_copy(j).start()
     for y in range(years_dev):
         beyond = dual_r[0, y].astype(jnp.float32)
         for k in range(2, hours):
@@ -380,10 +406,12 @@
         @pl.when(jnp.logical_or(me_h + k == hours - 1, jnp.logical_and(me_h + k < hours, me_l == 1)))
         def _(k=k):
             bar_copy(k).start()
-    for j in range(1, years):
-        @pl.when(jnp.logical_and(me_h < hours - 1, me_y + j < years))
-        def _(j=j):
-            above_copy(j).start()
+    for r in range(rows):
+        part = bal_s[r]
+        for b in range(0, store_rows, 8):
+            part = part - sbar_v[r, b : b + 8]
+        bal_s[r] = part
+    bal_copy.start()
     total_v[...] = total_v[...] + above
     place(sbar_v, -1.0, 0, store_rows, placed_v[...], placed_v)
 
@@ -393,14 +421,6 @@
             inj_s[r] = inject_part(r)
         inj_copy.start()
 
-    for r in range(rows):
-        part = None
-        for b in range(0, gen_rows, 8):
-            part = gbar_v[r, b : b + 8] if part is None else part + gbar_v[r, b : b + 8]
-        for b in range(0, store_rows, 8):
-            part = part - sbar_v[r, b : b + 8]
-        bal_s[r] = part
-    bal_copy.start()
 
     for c in range(line_local // LANES):
         limit1[:, c * LANES : (c + 1) * LANES] = limit_v[c : c + 1, :]
@@ -408,6 +428,8 @@
 
     @pl.when(me_l == 1)
     def _():
+        arrive(sent.at[pl.ds(0, (2 * rows + 2) * store_rows)], recv_sem.at[4])
+        encode(mate_node, store_rows + gen_rows, store_rows)
         for count in range(1, hours):
             @pl.when(me_h + count == hours - 1)
             def _(count=count):
@@ -442,9 +464,9 @@
         def lines_group(accs, first=first):
             group = range(first, min(first + THIN, line_tiles))
             multiply([
-                (k % 2, accs[k % 2][n - first], inject_half[:, cols(k)], tile(k, n))
+                (k % 2, accs[k % 2][n - first], inject_half[:, cols(k)], wide(ptdf_t.at[k, n], 0, 2))
                 for n in group for k in range(node_tiles)
-            ], True)
+            ], False)
             for i, n in enumerate(group):
                 line8[:, cols(n)] = pltpu.matmul_pop(accs[0][i]) + pltpu.matmul_pop(accs[1][i])
 
@@ -581,6 +603,7 @@
         pltpu.VMEM(block, jnp.int32), pltpu.VMEM((rows,) + block, f32), pltpu.VMEM((years_dev,) + block, LINK),
         pltpu.VMEM((h1, years_dev) + block, LINK),
         pltpu.VMEM((rows, 8, LANES), f32), pltpu.VMEM((rows, 8, LANES), f32),
+        pltpu.VMEM((nodes // TILE, line_local // TILE, 2, TILE, LANES), ptdf.dtype),
         dma((2,)), dma, dma((8,)), pltpu.SemaphoreType.REGULAR, pltpu.SemaphoreType.REGULAR,
     ]
     results = pl.pallas_call(

time: 10.9 us -> 10.7 us (0.982)
  Pallas kernels: 10.1 us -> 9.92 us
    pallas_call x1, Pallas kernels: 9.43 us -> 9.25 us  [local(): pl.pallas_call(functools.partial(step_kernel, sizes), out_shape=[pltpu.VM...]
where the time goes in v6:
time: 10.7 us; the launch traced here: 10.6 us
  Pallas kernels  9.92 us (93%)
  between operations  0.65 us (6%)
    pallas_call x1, Pallas kernels, local(): pl.pallas_call(functools.partial(step_kernel, sizes), out_shape=[pltpu.VM...  9.25 us
    pallas_call x1, Pallas kernels, local(): pl.pallas_call(functools.partial(finish_kernel, len(results)), out_shape=...  0.66 us

profile of v6, /device:TPU:0, one launch (start us, length us, event | category | flops | bytes accessed | tf_op | source)
XLA Modules:
  0.0 10.6 jit_solution(12960899815341609474)
XLA Ops:
  0.6 9.3 %shard_map.216 = (f32[2,16,128]{2,1,0:T(8,128)S(1)}, f32[2,32,128]{2,1,0:T(8,128)S(1)}, f32[32,128]{1,0:T(8,128)S(1)}, f32[2,1,768]{2,1,0:T(1,128)S(1)}, f32[2,3...) custom-call(bf16[2,2048]{1,0:T(2,128)(2,1)} %bitcast.29, bf16[2,2048]{1,0:T(2,128)(2,1)} %bitcast.30, ...), custom_call_target="tpu_custom_call" | custom-call | tf_op jit(solution)/shard_map/pallas_call | solution.py:609
  9.9 0.7 %shard_map.217 = (f32[2,16,128]{2,1,0:T(8,128)}, f32[2,32,128]{2,1,0:T(8,128)}, f32[32,128]{1,0:T(8,128)}, f32[2,1,768]{2,1,0:T(1,128)}, f32[2,32,128]{2,1,0:T(8...) custom-call(f32[2,16,128]{2,1,0:T(8,128)S(1)} %get-tuple-element.21.refs_0_, f32[2,32,128]{2,1,0:T(8,128)S(1)} %get-tuple-element.22.refs_1_, ...), custom_call_target="tpu_custom_call" | custom-call | tf_op jit(solution)/shard_map/pallas_call | solution.py:619

commit v7 on v6

--- a/solution.py
+++ b/solution.py
@@ -58,12 +58,21 @@
     def wide(ref, first, count):
         return jnp.concatenate([ref[first + i] for i in range(count)], axis=1)
 
-    def multiply(jobs, transpose):
-        stage = [0, 0]
-        for unit, acc, left, right in jobs:
-            pltpu.matmul_push_rhs(right, stage[unit], unit, transpose=transpose)
-            pltpu.matmul_acc_lhs(acc, left, load_staged_rhs=stage[unit])
-            stage[unit] = 1 - stage[unit]
+    def stage_first(rights, transpose):
+        for unit in range(2):
+            for i, right in enumerate(rights[unit][:2]):
+                pltpu.matmul_push_rhs(right, i, unit, transpose=transpose)
+
+    def multiply(jobs, transpose, staged=False):
+        split = [[job for job in jobs if job[0] == unit] for unit in range(2)]
+        if not staged:
+            stage_first([[job[3] for job in part] for part in split], transpose)
+        for i in range(max(len(part) for part in split)):
+            for unit, part in enumerate(split):
+                if i < len(part):
+                    pltpu.matmul_acc_lhs(part[i][1], part[i][2], load_staged_rhs=i % 2)
+                if i + 2 < len(part):
+                    pltpu.matmul_push_rhs(part[i + 2][3], i % 2, unit, transpose=transpose)
 
     def tile(i, rows_from):
         rows_here = pl.ds(rows_from * TILE, TILE)
@@ -178,11 +187,20 @@
             def _(k=k, j=j):
                 cross_copy(k, j).start()
     for k in range(hours - 1, 0, -1):
+        @pl.when(jnp.logical_and(jnp.logical_and(me_h == k, me_l == 0), me_y > 0))
+        def _(k=k):
+            mate_dual_copy(k).start()
+
         @pl.when(me_h >= k)
         def _(k=k):
             dual_copy(k).start()
 
-        @pl.when(jnp.logical_and(me_h >= k, me_l == 0))
+        @pl.when(jnp.logical_and(jnp.logical_and(me_h == k, me_l == 0), me_y == 0))
+        def _(k=k):
+            mate_dual_copy(k).start()
+
+    for k in range(hours - 1, 0, -1):
+        @pl.when(jnp.logical_and(me_h > k, me_l == 0))
         def _(k=k):
             mate_dual_copy(k).start()
     for j in range(1, years):
@@ -244,9 +262,9 @@
             avail_d[r, j : j + 1, :] = avail_v[r : r + 1, piece].astype(jnp.float32)
 
     diagonal = lax.broadcasted_iota(jnp.int32, (TILE, TILE), 0) == lax.broadcasted_iota(jnp.int32, (TILE, TILE), 1)
-    identity = jnp.where(diagonal, 1.0, 0.0).astype(jnp.bfloat16)
 
     def turn(accs):
+        identity = jnp.where(diagonal, 1.0, 0.0).astype(jnp.bfloat16)
         work = [(k, n) for k in range(node_tiles) for n in range(line_tiles)]
         held = 2 * DEPTH
         for i in range(len(work) + held):
@@ -260,7 +278,9 @@
                 pltpu.matmul_push_rhs(tile(k, n), (i // 2) % 2, i % 2, transpose=True)
                 pltpu.matmul_acc_lhs(accs[i % 2][(i // 2) % DEPTH], identity, load_staged_rhs=(i // 2) % 2)
 
-    scoped(TILE, DEPTH, turn)
+    @pl.when(me_l == 1)
+    def _():
+        scoped(TILE, DEPTH, turn)
 
     net_copy.wait_recv()
     prices = net_s[...] + net_r[...]
@@ -291,6 +311,7 @@
                 mate_s[r] = store_v[r] - TAU * (level_scale * own - price_v[r])
                 mate_s[rows + r] = store_v[r]
         mate_copy.start()
+        scoped(TILE, DEPTH, turn)
 
     for r in range(rows):
         for b in range(0, gen_rows, 8):
@@ -301,7 +322,10 @@
             gen_w[r, part] = new
             gbar_v[r, part] = 2.0 * new - gen_v[r, part]
 
-    def place(values, sign, first, count, start, target):
+    def place_tile(a):
+        return jnp.concatenate([wide(onehot, a, 2), wide(onehot, a + 2, 2)], axis=0)
+
+    def place(values, sign, first, count, start, target, staged=False):
         pieces = []
         for r in range(rows):
             rest = sign * values[r]
@@ -322,12 +346,11 @@
         jobs = []
         for t in range(count // 4):
             left = jnp.concatenate([pair(spread, 4 * t), pair(spread, 4 * t + 2)], axis=0)
-            right = jnp.concatenate([wide(onehot, first + 4 * t, 2), wide(onehot, first + 4 * t + 2, 2)], axis=0)
-            jobs.append((t % 2, left, right))
+            jobs.append((t % 2, left, place_tile(first + 4 * t)))
         height = rows * SPLITS * hi_count
 
         def finish(accs):
-            multiply([(i, accs[i][0], left, right) for i, left, right in jobs], True)
+            multiply([(i, accs[i][0], left, right) for i, left, right in jobs], True, staged)
             for i in range(2):
                 both = pltpu.matmul_pop(accs[i][0])
                 part = both[:height, :LANES] + both[height:, LANES:]
@@ -372,6 +395,9 @@
             @pl.when(me_h + k < hours)
             def _(k=k):
                 up_copy(k).start()
+
+    store_tiles = range(store_rows // 4)
+    stage_first([[place_tile(4 * t) for t in store_tiles if t % 2 == unit] for unit in range(2)], True)
 
     for count in range(1, hours):
         @pl.when(me_h + count == hours - 1)
@@ -403,7 +429,7 @@
             bar_total = sbar if bar_total is None else bar_total + sbar
         bar_s[y] = bar_total.astype(link)
     for k in range(hours - 1, 0, -1):
-        @pl.when(jnp.logical_or(me_h + k == hours - 1, jnp.logical_and(me_h + k < hours, me_l == 1)))
+        @pl.when(jnp.logical_and(me_h + k < hours, jnp.logical_or(me_h > 0, me_l == 1)))
         def _(k=k):
             bar_copy(k).start()
     for r in range(rows):
@@ -413,7 +439,7 @@
         bal_s[r] = part
     bal_copy.start()
     total_v[...] = total_v[...] + above
-    place(sbar_v, -1.0, 0, store_rows, placed_v[...], placed_v)
+    place(sbar_v, -1.0, 0, store_rows, placed_v[...], placed_v, True)
 
     @pl.when(me_l == 1)
     def _():
@@ -448,8 +474,8 @@
                 mate_bar[r] = sbar
                 bar_total = sbar if bar_total is None else bar_total + sbar
             mate_sum[y] = bar_total.astype(link)
-        for k in range(hours - 2, 0, -1):
-            @pl.when(me_h + k < hours - 1)
+        for k in range(hours - 1, 0, -1):
+            @pl.when(me_h == 0)
             def _(k=k):
                 mate_bar_copy(k).start()
         place(mate_bar, -1.0, store_rows + gen_rows, store_rows, placed_v[...], placed_v)
@@ -517,8 +543,8 @@
     for y in range(years):
         for h in range(hours):
             blocks = h * years_dev + h * y + (years - 1 - y if h < hours - 1 else 0)
-            near = years_dev * (h + (1 if h < hours - 1 else 0))
-            far = years_dev * (hours - 1 - h + max(hours - 2 - h, 0))
+            near = years_dev * (h + (hours - 1 - h if h > 0 else 0))
+            far = years_dev * (hours - 1 - h + (hours - 1 if h == 0 else 0))
             extra = (2 * rows + 2) * store_rows
 
             @pl.when(jnp.logical_and(jnp.logical_and(me_h == h, me_y == y), me_l == 0))

time: 10.7 us -> 10.6 us (level)
  no operation moved by 1% of the time
where the time goes in v7:
time: 10.6 us; the launch traced here: 10.5 us
  Pallas kernels  9.82 us (93%)
  between operations  0.65 us (6%)
    pallas_call x1, Pallas kernels, local(): pl.pallas_call(functools.partial(step_kernel, sizes), out_shape=[pltpu.VM...  9.15 us
    pallas_call x1, Pallas kernels, local(): pl.pallas_call(functools.partial(finish_kernel, len(results)), out_shape=...  0.66 us

profile of v7, /device:TPU:0, one launch (start us, length us, event | category | flops | bytes accessed | tf_op | source)
XLA Modules:
  0.0 10.5 jit_solution(404547044467492103)
XLA Ops:
  0.6 9.2 %shard_map.216 = (f32[2,16,128]{2,1,0:T(8,128)S(1)}, f32[2,32,128]{2,1,0:T(8,128)S(1)}, f32[32,128]{1,0:T(8,128)S(1)}, f32[2,1,768]{2,1,0:T(1,128)S(1)}, f32[2,3...) custom-call(bf16[2,2048]{1,0:T(2,128)(2,1)} %bitcast.29, bf16[2,2048]{1,0:T(2,128)(2,1)} %bitcast.30, ...), custom_call_target="tpu_custom_call" | custom-call | tf_op jit(solution)/shard_map/pallas_call | solution.py:635
  9.8 0.7 %shard_map.217 = (f32[2,16,128]{2,1,0:T(8,128)}, f32[2,32,128]{2,1,0:T(8,128)}, f32[32,128]{1,0:T(8,128)}, f32[2,1,768]{2,1,0:T(1,128)}, f32[2,32,128]{2,1,0:T(8...) custom-call(f32[2,16,128]{2,1,0:T(8,128)S(1)} %get-tuple-element.21.refs_0_, f32[2,32,128]{2,1,0:T(8,128)S(1)} %get-tuple-element.22.refs_1_, ...), custom_call_target="tpu_custom_call" | custom-call | tf_op jit(solution)/shard_map/pallas_call | solution.py:645

commit v8 on v6

--- a/solution.py
+++ b/solution.py
@@ -178,11 +178,20 @@
             def _(k=k, j=j):
                 cross_copy(k, j).start()
     for k in range(hours - 1, 0, -1):
+        @pl.when(jnp.logical_and(jnp.logical_and(me_h == k, me_l == 0), me_y > 0))
+        def _(k=k):
+            mate_dual_copy(k).start()
+
         @pl.when(me_h >= k)
         def _(k=k):
             dual_copy(k).start()
 
-        @pl.when(jnp.logical_and(me_h >= k, me_l == 0))
+        @pl.when(jnp.logical_and(jnp.logical_and(me_h == k, me_l == 0), me_y == 0))
+        def _(k=k):
+            mate_dual_copy(k).start()
+
+    for k in range(hours - 1, 0, -1):
+        @pl.when(jnp.logical_and(me_h > k, me_l == 0))
         def _(k=k):
             mate_dual_copy(k).start()
     for j in range(1, years):
@@ -244,9 +253,9 @@
             avail_d[r, j : j + 1, :] = avail_v[r : r + 1, piece].astype(jnp.float32)
 
     diagonal = lax.broadcasted_iota(jnp.int32, (TILE, TILE), 0) == lax.broadcasted_iota(jnp.int32, (TILE, TILE), 1)
-    identity = jnp.where(diagonal, 1.0, 0.0).astype(jnp.bfloat16)
 
     def turn(accs):
+        identity = jnp.where(diagonal, 1.0, 0.0).astype(jnp.bfloat16)
         work = [(k, n) for k in range(node_tiles) for n in range(line_tiles)]
         held = 2 * DEPTH
         for i in range(len(work) + held):
@@ -260,7 +269,9 @@
                 pltpu.matmul_push_rhs(tile(k, n), (i // 2) % 2, i % 2, transpose=True)
                 pltpu.matmul_acc_lhs(accs[i % 2][(i // 2) % DEPTH], identity, load_staged_rhs=(i // 2) % 2)
 
-    scoped(TILE, DEPTH, turn)
+    @pl.when(me_l == 1)
+    def _():
+        scoped(TILE, DEPTH, turn)
 
     net_copy.wait_recv()
     prices = net_s[...] + net_r[...]
@@ -291,6 +302,7 @@
                 mate_s[r] = store_v[r] - TAU * (level_scale * own - price_v[r])
                 mate_s[rows + r] = store_v[r]
         mate_copy.start()
+        scoped(TILE, DEPTH, turn)
 
     for r in range(rows):
         for b in range(0, gen_rows, 8):
@@ -403,7 +415,7 @@
             bar_total = sbar if bar_total is None else bar_total + sbar
         bar_s[y] = bar_total.astype(link)
     for k in range(hours - 1, 0, -1):
-        @pl.when(jnp.logical_or(me_h + k == hours - 1, jnp.logical_and(me_h + k < hours, me_l == 1)))
+        @pl.when(jnp.logical_and(me_h + k < hours, jnp.logical_or(me_h > 0, me_l == 1)))
         def _(k=k):
             bar_copy(k).start()
     for r in range(rows):
@@ -448,8 +460,8 @@
                 mate_bar[r] = sbar
                 bar_total = sbar if bar_total is None else bar_total + sbar
             mate_sum[y] = bar_total.astype(link)
-        for k in range(hours - 2, 0, -1):
-            @pl.when(me_h + k < hours - 1)
+        for k in range(hours - 1, 0, -1):
+            @pl.when(me_h == 0)
             def _(k=k):
                 mate_bar_copy(k).start()
         place(mate_bar, -1.0, store_rows + gen_rows, store_rows, placed_v[...], placed_v)
@@ -517,8 +529,8 @@
     for y in range(years):
         for h in range(hours):
             blocks = h * years_dev + h * y + (years - 1 - y if h < hours - 1 else 0)
-            near = years_dev * (h + (1 if h < hours - 1 else 0))
-            far = years_dev * (hours - 1 - h + max(hours - 2 - h, 0))
+            near = years_dev * (h + (hours - 1 - h if h > 0 else 0))
+            far = years_dev * (hours - 1 - h + (hours - 1 if h == 0 else 0))
             extra = (2 * rows + 2) * store_rows
 
             @pl.when(jnp.logical_and(jnp.logical_and(me_h == h, me_y == y), me_l == 0))

time: 10.7 us -> 10.6 us (level)
  no operation moved by 1% of the time
where the time goes in v8:
time: 10.6 us; the launch traced here: 10.5 us
  Pallas kernels  9.82 us (93%)
  between operations  0.65 us (6%)
    pallas_call x1, Pallas kernels, local(): pl.pallas_call(functools.partial(step_kernel, sizes), out_shape=[pltpu.VM...  9.15 us
    pallas_call x1, Pallas kernels, local(): pl.pallas_call(functools.partial(finish_kernel, len(results)), out_shape=...  0.66 us

profile of v8, /device:TPU:0, one launch (start us, length us, event | category | flops | bytes accessed | tf_op | source)
XLA Modules:
  0.0 10.5 jit_solution(2012642046208239995)
XLA Ops:
  0.6 9.2 %shard_map.216 = (f32[2,16,128]{2,1,0:T(8,128)S(1)}, f32[2,32,128]{2,1,0:T(8,128)S(1)}, f32[32,128]{1,0:T(8,128)S(1)}, f32[2,1,768]{2,1,0:T(1,128)S(1)}, f32[2,3...) custom-call(bf16[2,2048]{1,0:T(2,128)(2,1)} %bitcast.29, bf16[2,2048]{1,0:T(2,128)(2,1)} %bitcast.30, ...), custom_call_target="tpu_custom_call" | custom-call | tf_op jit(solution)/shard_map/pallas_call | solution.py:621
  9.8 0.7 %shard_map.217 = (f32[2,16,128]{2,1,0:T(8,128)}, f32[2,32,128]{2,1,0:T(8,128)}, f32[32,128]{1,0:T(8,128)}, f32[2,1,768]{2,1,0:T(1,128)}, f32[2,32,128]{2,1,0:T(8...) custom-call(f32[2,16,128]{2,1,0:T(8,128)S(1)} %get-tuple-element.21.refs_0_, f32[2,32,128]{2,1,0:T(8,128)S(1)} %get-tuple-element.22.refs_1_, ...), custom_call_target="tpu_custom_call" | custom-call | tf_op jit(solution)/shard_map/pallas_call | solution.py:631
